TPU v7x, 128 devices: a whole 4x4x4 slice. The times are simulated.
128 devices in a mesh: gx: 8 (over x_lo, y), gy: 16 (over x_hi, z, core).
Axes of the slice: x: 4 (x_hi: 2, x_lo: 2; x = x_hi * 2 + x_lo), y: 4, z: 4, core: 2. Of those that a mesh axis runs over, the one named last changes fastest.
Arguments:
- east_wind: bfloat16 [4096, 4096], P('gy', 'gx'), may hold values from -6 to 6
- north_wind: bfloat16 [4096, 4096], P('gy', 'gx'), may hold values from -6 to 6
- height: bfloat16 [4096, 4096], P('gy', 'gx'), may hold values from -6 to 6
- tracer: bfloat16 [4096, 4096], P('gy', 'gx'), may hold values from -6 to 6
Outputs:
- east_next: bfloat16 [4096, 4096], P('gy', 'gx')
- north_next: bfloat16 [4096, 4096], P('gy', 'gx')
- height_next: bfloat16 [4096, 4096], P('gy', 'gx')
- tracer_next: bfloat16 [4096, 4096], P('gy', 'gx')
All inputs are finite; a program needn't handle non-finite values.
Results may differ from a plain program's by a relative error of at most 0.0014.
Values may be sent and summed in bfloat16 or wider, within the bound.
A program may use at most 128 MiB of HBM per device.

v0:
```python
import math

import jax
import jax.numpy as jnp
import numpy as np
from jax import lax
from jax.experimental import pallas as pl
from jax.experimental.pallas import tpu as pltpu
from jax.sharding import PartitionSpec as P

NG = 4096
FIELDS = 4
GX = 8
GY = 16
DEVICES = GX * GY
KX = 11
SLAB = 24
ROWS = 32
COLS = 512
POWER = 11

coriolis = 0.25
gravity_step = 2.0
depth_step = 2.0
diffusion = 0.02

F32 = jnp.float32
BF16 = jnp.bfloat16
MESH = pl.DeviceIdType.MESH


def split_const(matrix):
    whole = matrix.astype(np.float32)
    high = np.dtype(jnp.bfloat16)
    head = whole.astype(high)
    tail = (whole - head.astype(np.float32)).astype(high)
    return head, tail


def wave_of(slot, place):
    if slot == 0:
        return 32 * place if place < 43 else 16 + 32 * (place - 43)
    return slot + 32 * (place - 43)


def tables():
    turn = 2.0 * np.pi
    lane = np.arange(128)
    forward = np.zeros((2, GX, 2, SLAB // 2, 256))
    inverse = np.zeros((2, GX, 2, SLAB // 2, 256))
    for place in range(86):
        octant, member = place // KX, place % KX
        low = place - 43
        cosine, sine = np.cos(turn * lane * low / 128), np.sin(turn * lane * low / 128)
        forward[1, octant, 0, member] = np.concatenate([cosine, sine])
        forward[1, octant, 1, member] = np.concatenate([-sine, cosine])
        inverse[1, octant, 0, member] = np.concatenate([cosine, sine])
        inverse[1, octant, 1, member] = np.concatenate([-sine, cosine])
        wave = wave_of(0, place)
        cosine, sine = np.cos(turn * lane * wave / NG), np.sin(turn * lane * wave / NG)
        half = 0 if place < 43 else 128
        weight = 1.0 if wave == 0 else 2.0
        forward[0, octant, 0, member, half : half + 128] = cosine
        forward[0, octant, 1, member, half : half + 128] = -sine
        inverse[0, octant, 0, member, half : half + 128] = weight * cosine
        inverse[0, octant, 1, member, half : half + 128] = -weight * sine
    forward = forward.reshape(2, GX * SLAB, 256)
    inverse = inverse.reshape(2, GX * SLAB, 256)
    angle = turn * np.outer(np.arange(GY), lane) / NG
    twist = np.stack([np.cos(angle), np.sin(angle)], axis=1)[:, :, None, :]
    twist = np.broadcast_to(twist, (GY, 2, 16, 128)).astype(np.float32)
    angle = turn * np.outer(lane, lane) / 128
    cosine, sine = np.cos(angle), np.sin(angle)
    gather = np.block([[cosine, sine], [-sine, cosine]])
    scatter = np.block([[cosine, -sine], [sine, cosine]])
    angle = turn * np.outer(np.arange(ROWS), np.arange(ROWS)) / ROWS
    cosine, sine = np.kron(np.eye(4), np.cos(angle)), np.kron(np.eye(4), np.sin(angle))
    fan_in = np.block([[cosine, -sine], [sine, cosine]])
    fan_out = np.block([[cosine, sine], [-sine, cosine]])
    angle = turn * np.outer(lane, lane % ROWS) / NG
    spin = np.stack([np.cos(angle), np.sin(angle)]).astype(np.float32)
    pairs = []
    for matrix in (forward, inverse, gather, scatter, fan_in, fan_out):
        pairs.extend(split_const(matrix))
    return pairs + [twist, spin]


def real_transform(values):
    count = len(values)
    if count == 2:
        return [(values[0] + values[1], None), (values[0] - values[1], None)]
    even = real_transform(values[0::2])
    odd = real_transform(values[1::2])
    half = count // 2
    result = [None] * (half + 1)
    for index in range(count // 4 + 1):
        even_real, even_imag = even[index]
        odd_real, odd_imag = odd[index]
        if index == 0:
            result[0] = (even_real + odd_real, None)
            result[half] = (even_real - odd_real, None)
        elif index == count // 4:
            result[index] = (even_real, -odd_real)
        else:
            cosine = math.cos(2.0 * math.pi * index / count)
            sine = math.sin(2.0 * math.pi * index / count)
            turned_real = odd_real * cosine + odd_imag * sine
            turned_imag = odd_imag * cosine - odd_real * sine
            result[index] = (even_real + turned_real, even_imag + turned_imag)
            result[half - index] = (even_real - turned_real, turned_imag - even_imag)
    return result


def real_inverse(waves):
    half = len(waves) - 1
    count = 2 * half
    if count == 2:
        return [waves[0][0] + waves[1][0], waves[0][0] - waves[1][0]]
    even = []
    odd = []
    for index in range(count // 4 + 1):
        real, imag = waves[index]
        other_real, other_imag = waves[half - index]
        if index == 0:
            even.append((real + other_real, None))
            odd.append((real - other_real, None))
        elif index == count // 4:
            even.append((real + real, None))
            odd.append((-(imag + imag), None))
        else:
            cosine = math.cos(2.0 * math.pi * index / count)
            sine = math.sin(2.0 * math.pi * index / count)
            even.append((real + other_real, imag - other_imag))
            gap_real = real - other_real
            gap_imag = imag + other_imag
            odd.append((gap_real * cosine - gap_imag * sine, gap_real * sine + gap_imag * cosine))
    outputs = [None] * count
    outputs[0::2] = real_inverse(even)
    outputs[1::2] = real_inverse(odd)
    return outputs


def parts(values):
    head = values.astype(BF16)
    return head, (values - head.astype(F32)).astype(BF16)


def product(left, right, dims):
    return lax.dot_general(left, right, (dims, ((), ())), preferred_element_type=F32)


def product3(left, right, dims):
    left_head, left_tail = left
    right_head, right_tail = right
    return (
        product(left_head, right_head, dims)
        + product(left_head, right_tail, dims)
        + product(left_tail, right_head, dims)
    )


NN = ((1,), (0,))
NT = ((1,), (1,))
TN = ((0,), (0,))


def fill_gains(gains, octant, slot):
    chunk = 32

    def body(step, carry):
        member = step // (128 // chunk)
        top = (step % (128 // chunk)) * chunk
        place = KX * octant + member
        zero_slot = jnp.where(place < 43, 32 * place, 16 + 32 * (place - 43))
        mode_x = jnp.where(slot == 0, zero_slot, slot + 32 * (place - 43))
        lane = lax.broadcasted_iota(jnp.int32, (chunk, 128), 1)
        row = lax.broadcasted_iota(jnp.int32, (chunk, 128), 0) + top
        field = lane // 32
        mode_y = row + 128 * (lane % 32)
        mode_y = jnp.where(mode_y < NG // 2, mode_y, mode_y - NG)
        cutoff = NG // 3
        inside = mode_y * mode_y + mode_x * mode_x <= cutoff * cutoff
        unit = 2.0 * math.pi / NG
        wave_x = mode_x.astype(F32) * unit
        wave_y = mode_y.astype(F32) * unit
        square = wave_x * wave_x + wave_y * wave_y
        scale = 1.0 / (NG * NG)
        gain = jnp.where(inside, scale / (1.0 + diffusion * square * square), 0.0)
        stiffness = gravity_step * depth_step * square
        below = 1.0 / (1.0 + coriolis * coriolis + stiffness)
        above = (1.0 - coriolis * coriolis - stiffness) * below
        twice = (2.0 * coriolis) * below
        push_u = above * wave_x - twice * wave_y
        push_v = above * wave_y + twice * wave_x
        push_h = (2.0 * gravity_step) * square * below
        sum_u = wave_x + push_u
        sum_v = wave_y + push_v
        curl_u = -wave_y - coriolis * sum_u
        curl_v = wave_x - coriolis * sum_v
        curl_h = -coriolis * push_h
        anchor = square == 0.0
        over = 1.0 / jnp.where(anchor, 1.0, square)
        first = field == 0
        second = field == 1
        third = field == 2
        lead = jnp.where(first, -wave_y, wave_x)
        trail = jnp.where(first, wave_x, wave_y)
        from_u = (lead * curl_u + trail * push_u) * over
        from_v = (lead * curl_v + trail * push_v) * over
        from_h = -(lead * curl_h + trail * push_h) * over
        rotate = 1.0 / (1.0 + coriolis * coriolis)
        keep = (1.0 - coriolis * coriolis) * rotate
        cross = 2.0 * coriolis * rotate
        from_u = jnp.where(anchor, jnp.where(first, keep, -cross), from_u)
        from_v = jnp.where(anchor, jnp.where(first, cross, keep), from_v)
        zero = jnp.zeros_like(gain)
        same = jnp.where(
            first,
            from_u,
            jnp.where(second, from_v, jnp.where(third, 1.0 - depth_step * push_h, 1.0)),
        )
        one = jnp.where(second, from_u, jnp.where(third, -depth_step * sum_v, zero))
        two = jnp.where(first, from_h, jnp.where(third, -depth_step * sum_u, zero))
        three = jnp.where(first, from_v, jnp.where(second, from_h, zero))
        place_rows = pl.ds(pl.multiple_of(top, chunk), chunk)
        gains[member, 0, place_rows, :] = same * gain
        gains[member, 1, place_rows, :] = one * gain
        gains[member, 2, place_rows, :] = two * gain
        gains[member, 3, place_rows, :] = three * gain
        return carry

    lax.fori_loop(0, KX * (128 // chunk), body, 0)


def apply_gains(gains, member, real, imag):
    lane = lax.broadcasted_iota(jnp.int32, (128, 128), 1)
    field = lane // 32
    second = field == 1
    third = field == 2
    gain = gains[member, 0]
    out_real = real * gain
    out_imag = imag * gain
    crossed = [third, None, second]
    for turn in (1, 2, 3):
        gain = gains[member, turn]
        moved_real = pltpu.roll(real, 32 * turn, 1)
        moved_imag = pltpu.roll(imag, 32 * turn, 1)
        swap = crossed[turn - 1]
        if swap is None:
            use_real, use_imag = -moved_imag, moved_real
        else:
            use_real = jnp.where(swap, -moved_imag, moved_real)
            use_imag = jnp.where(swap, moved_real, moved_imag)
        out_real = out_real + gain * use_real
        out_imag = out_imag + gain * use_imag
    return out_real, out_imag


def step_kernel(*refs):
    sources = refs[0:4]
    (fwd_h, fwd_l, inv_h, inv_l, gat_h, gat_l, sca_h, sca_l, fin_h, fin_l, fout_h, fout_l) = refs[4:16]
    twist, spin = refs[16:18]
    results = refs[18:22]
    (
        grid_rows,
        head,
        tail,
        slabs,
        landed,
        columns,
        gains,
        returned,
        waves,
        new_rows,
        sem_rows_out,
        sem_rows_in,
        sem_out,
        sem_in,
        sem_back_out,
        sem_back_in,
        sem_last_out,
        sem_last_in,
    ) = refs[22:]
    octant = lax.axis_index("gx")
    slot_own = lax.axis_index("gy")
    own = slot_own * GX + octant

    barrier = pltpu.get_barrier_semaphore()

    def greet(step, carry):
        other = (own + step) % DEVICES
        pl.semaphore_signal(
            barrier, inc=1, device_id=(other % GX, other // GX), device_id_type=MESH
        )
        return carry

    lax.fori_loop(1, DEVICES, greet, 0)
    fill_gains(gains, octant, slot_own)
    pl.semaphore_wait(barrier, DEVICES - 1)

    for field in range(FIELDS):
        for step in range(1, GX):
            other = (octant + step) % GX
            pltpu.make_async_remote_copy(
                src_ref=sources[field].at[pl.ds(pl.multiple_of(other * ROWS, ROWS), ROWS), :],
                dst_ref=grid_rows.at[field, octant],
                send_sem=sem_rows_out.at[field],
                recv_sem=sem_rows_in.at[field],
                device_id=(other, slot_own),
                device_id_type=MESH,
            ).start()
        pltpu.make_async_copy(
            sources[field].at[pl.ds(pl.multiple_of(octant * ROWS, ROWS), ROWS), :],
            grid_rows.at[field, octant],
            sem_rows_in.at[field],
        ).start()

    def row_body(step, carry):
        field = step // 2
        part = step % 2
        top = pl.multiple_of(part * 16, 16)
        chunk = [
            grid_rows[field, c // 4, pl.ds(top, 16), (c % 4) * 128 : (c % 4) * 128 + 128].astype(F32)
            for c in range(32)
        ]
        spectrum = real_transform(chunk)
        rows = pl.ds(pl.multiple_of(step * 16, 16), 16)
        for slot in range(GY):
            if slot == 0:
                real, imag = spectrum[0][0], spectrum[16][0]
            else:
                wave_real, wave_imag = spectrum[slot]
                cosine, sine = twist[slot, 0], twist[slot, 1]
                real = wave_real * cosine + wave_imag * sine
                imag = wave_imag * cosine - wave_real * sine
            for side, value in ((0, real), (128, imag)):
                high, low = parts(value)
                head[slot, rows, side : side + 128] = high
                tail[slot, rows, side : side + 128] = low
        return carry

    for field in range(FIELDS):
        pltpu.make_async_copy(
            grid_rows.at[field], grid_rows.at[field], sem_rows_in.at[field]
        ).wait()
        lax.fori_loop(2 * field, 2 * field + 2, row_body, 0)

    def send(place, target, out_sem, in_sem):
        pltpu.make_async_remote_copy(
            src_ref=slabs.at[place],
            dst_ref=target.at[own],
            send_sem=out_sem,
            recv_sem=in_sem,
            device_id=(place % GX, place // GX),
            device_id_type=MESH,
        ).start()

    def slot_product(slot):
        which = (slot + GY - 1) // GY
        spectrum = product3(
            (fwd_h[which], fwd_l[which]), (head[slot], tail[slot]), NT
        )
        slabs[pl.ds(pl.multiple_of(slot * GX, GX), GX)] = spectrum.reshape(GX, SLAB, 128)

    slot_product(slot_own)
    for step in range(1, GX):
        send(slot_own * GX + (octant + step) % GX, landed, sem_out, sem_in)
    pltpu.make_async_copy(slabs.at[own], landed.at[own], sem_in).start()

    def slot_body(step, carry):
        slot = (slot_own + step) % GY
        slot_product(slot)
        for other in range(GX):
            send(slot * GX + (octant + other) % GX, landed, sem_out, sem_in)
        return carry

    lax.fori_loop(1, GY, slot_body, 0)

    pltpu.make_async_copy(landed, landed, sem_in).wait()

    def spread(source, carry):
        columns[pl.ds(source, SLAB, stride=128), :] = landed[source]
        return carry

    lax.fori_loop(0, DEVICES, spread, 0)

    def column_body(member, carry):
        real_rows = pl.ds(pl.multiple_of(member * 128, 128), 128)
        imag_rows = pl.ds(pl.multiple_of((member + SLAB // 2) * 128, 128), 128)
        values = jnp.concatenate([columns[real_rows, :], columns[imag_rows, :]], axis=0)
        mixed = product3((gat_h[...], gat_l[...]), parts(values), NN)
        real, imag = mixed[:128], mixed[128:]
        cosine, sine = spin[0], spin[1]
        turned = jnp.concatenate(
            [real * cosine + imag * sine, imag * cosine - real * sine], axis=1
        )
        modes = product3(parts(turned), (fin_h[...], fin_l[...]), NN)
        real, imag = apply_gains(gains, member, modes[:, :128], modes[:, 128:])
        modes = jnp.concatenate([real, imag], axis=1)
        mixed = product3(parts(modes), (fout_h[...], fout_l[...]), NN)
        real, imag = mixed[:, :128], mixed[:, 128:]
        values = jnp.concatenate(
            [real * cosine - imag * sine, imag * cosine + real * sine], axis=0
        )
        values = product3((sca_h[...], sca_l[...]), parts(values), NN)
        columns[real_rows, :] = values[:128]
        columns[imag_rows, :] = values[128:]
        return carry

    lax.fori_loop(0, KX, column_body, 0)

    sent = slabs.at[pl.ds(0, DEVICES - 1)]
    pltpu.make_async_copy(sent, sent, sem_out).wait()

    def collect(place):
        slabs[place] = columns[pl.ds(place, SLAB, stride=128), :]

    collect(own)
    pltpu.make_async_copy(slabs.at[own], returned.at[own], sem_back_in).start()

    def back_body(step, carry):
        place = (own + step) % DEVICES
        collect(place)
        send(place, returned, sem_back_out, sem_back_in)
        return carry

    lax.fori_loop(1, DEVICES, back_body, 0)
    pltpu.make_async_copy(returned, returned, sem_back_in).wait()

    def wave_body(slot, carry):
        which = (slot + GY - 1) // GY
        block = returned[pl.ds(pl.multiple_of(slot * GX, GX), GX)].reshape(GX * SLAB, 128)
        values = product3(parts(block), (inv_h[which], inv_l[which]), TN)
        real, imag = values[:, :128], values[:, 128:]
        cosine, sine = twist[slot, 0, 0:1, :], twist[slot, 1, 0:1, :]
        waves[slot, :, 0:128] = real * cosine - imag * sine
        waves[slot, :, 128:256] = imag * cosine + real * sine
        return carry

    lax.fori_loop(0, GY, wave_body, 0)

    def grid_body(step, carry):
        field = step // 2
        part = step % 2
        rows = pl.ds(pl.multiple_of(step * 16, 16), 16)
        spectrum = [(waves[0, rows, 0:128], None)]
        for slot in range(1, GY):
            spectrum.append((waves[slot, rows, 0:128], waves[slot, rows, 128:256]))
        spectrum.append((waves[0, rows, 128:256], None))
        values = real_inverse(spectrum)
        top = pl.ds(pl.multiple_of(part * 16, 16), 16)
        for c in range(32):
            new_rows[field, c // 4, top, (c % 4) * 128 : (c % 4) * 128 + 128] = values[c].astype(BF16)
        return carry

    for field in range(FIELDS):
        lax.fori_loop(2 * field, 2 * field + 2, grid_body, 0)
        own_rows = pl.ds(pl.multiple_of(octant * ROWS, ROWS), ROWS)
        for step in range(1, GX):
            other = (octant + step) % GX
            pltpu.make_async_remote_copy(
                src_ref=new_rows.at[field, other],
                dst_ref=results[field].at[own_rows, :],
                send_sem=sem_last_out.at[field],
                recv_sem=sem_last_in.at[field],
                device_id=(other, slot_own),
                device_id_type=MESH,
            ).start()
        pltpu.make_async_copy(
            new_rows.at[field, octant], results[field].at[own_rows, :], sem_last_in.at[field]
        ).start()

    sent = slabs.at[pl.ds(0, DEVICES - 1)]
    pltpu.make_async_copy(sent, sent, sem_back_out).wait()
    for field in range(FIELDS):
        moved = new_rows.at[field, pl.ds(0, GX - 1)]
        pltpu.make_async_copy(moved, moved, sem_rows_out.at[field]).wait()
        pltpu.make_async_copy(moved, moved, sem_last_out.at[field]).wait()
        pltpu.make_async_copy(results[field], results[field], sem_last_in.at[field]).wait()


def per_device(east_wind, north_wind, height, tracer):
    constants = [jnp.asarray(value) for value in tables()]
    anywhere = pl.BlockSpec(memory_space=pl.ANY)
    vmem = pl.BlockSpec(memory_space=pltpu.VMEM)
    block = jax.ShapeDtypeStruct((NG // GY, COLS), BF16)
    dma = pltpu.SemaphoreType.DMA
    return pl.pallas_call(
        step_kernel,
        out_shape=(block,) * 4,
        in_specs=[anywhere] * 4 + [vmem] * len(constants),
        out_specs=(anywhere,) * 4,
        scratch_shapes=[
            pltpu.VMEM((FIELDS, GX, ROWS, COLS), BF16),
            pltpu.VMEM((GY, 128, 256), BF16),
            pltpu.VMEM((GY, 128, 256), BF16),
            pltpu.VMEM((DEVICES, SLAB, 128), F32),
            pltpu.VMEM((DEVICES, SLAB, 128), F32),
            pltpu.VMEM((SLAB * 128, 128), F32),
            pltpu.VMEM((KX, 4, 128, 128), F32),
            pltpu.VMEM((DEVICES, SLAB, 128), F32),
            pltpu.VMEM((GY, 128, 256), F32),
            pltpu.VMEM((FIELDS, GX, ROWS, COLS), BF16),
            dma((FIELDS,)),
            dma((FIELDS,)),
            dma,
            dma,
            dma,
            dma,
            dma((FIELDS,)),
            dma((FIELDS,)),
        ],
        compiler_params=pltpu.CompilerParams(collective_id=0, has_side_effects=True),
    )(east_wind, north_wind, height, tracer, *constants)


def solution(mesh):
    placed = (P("gy", "gx"),) * 4
    return jax.shard_map(
        per_device, mesh=mesh, in_specs=placed, out_specs=placed, check_vma=False
    )
```

profile of v0, /device:TPU:1, one launch (start us, length us, event | category | flops | bytes accessed | tf_op | source)
XLA Modules:
  0.0 107.8 jit_solution(1393049545254168879)
XLA Ops:
  0.6 102.6 %shard_map.201 = (bf16[256,512]{1,0:T(8,128)(2,1)}, bf16[256,512]{1,0:T(8,128)(2,1)}, bf16[256,512]{1,0:T(8,128)(2,1)}, bf16[256,512]{1,0:T(8,128)(2,1)}) custom-call(bf16[256,512]{1,0:T(8,128)(2,1)} %refs_0_.1, bf16[256,512]{1,0:T(8,128)(2,1)} %refs_1_.1, bf16[256,512]{1,0:T(8,128)(2,1)} %refs_2_.1, bf16[256,512]{1,0:T(8,128)(2,1)} %refs_3_.1, ...), custom_call_target="tpu_custom_call" | custom-call | tf_op jit(solution)/shard_map/pallas_call | solution.py:488
  103.2 0.0 copy-start.2
  103.2 1.7 %copy.26 = bf16[256,512]{1,0:T(8,128)(2,1)} copy(bf16[256,512]{1,0:T(8,128)(2,1)} %get-tuple-element.8) | data formatting | bytes 524288
  105.0 0.0 copy-done.2
  105.0 0.0 copy-start.1
  105.0 0.7 copy.27
  105.7 0.3 copy-done.1
  106.0 0.0 copy-start
  106.0 0.7 copy.28
  106.7 0.3 copy-done
  107.0 0.7 copy.29
Async XLA Ops:
  103.2 1.7 %copy-start.2 = (bf16[256,512]{1,0:T(8,128)(2,1)S(1)}, bf16[256,512]{1,0:T(8,128)(2,1)}, u32[]{:S(2)}) copy-start(bf16[256,512]{1,0:T(8,128)(2,1)} %get-tuple-element.9) | copy-start | bytes 786436
  105.0 1.0 copy-start.1
  106.0 1.0 copy-start
where the time goes:
time: 108 us
  Pallas kernels  103 us (95%)
  local copies, waits for them, and re-layouts  4.5 us (4%)
    pallas_call x1, Pallas kernels, per_device(): pl.pallas_call(step_kernel, out_shape=(block,) * 4, in_specs=[anywhere] *...  103 us
    unnamed x10, local copies, waits for them, and re-layouts  4.5 us

commit v1 on v0

--- a/solution.py
+++ b/solution.py
@@ -79,10 +79,52 @@
     fan_out = np.block([[cosine, sine], [-sine, cosine]])
     angle = turn * np.outer(lane, lane % ROWS) / NG
     spin = np.stack([np.cos(angle), np.sin(angle)]).astype(np.float32)
-    pairs = []
-    for matrix in (forward, inverse, gather, scatter, fan_in, fan_out):
-        pairs.extend(split_const(matrix))
-    return pairs + [twist, spin]
+    pieces = []
+    for matrix in (forward.reshape(-1, 256), inverse.reshape(-1, 256) / NG, gather, scatter, fan_in, fan_out):
+        pieces.extend(split_const(matrix))
+    floats = np.concatenate([twist.reshape(-1, 128), spin.reshape(-1, 128)], axis=0)
+    return np.concatenate(pieces, axis=0), floats
+
+
+FWD_AT = 0
+INV_AT = 4 * GX * SLAB
+SQUARE_AT = 8 * GX * SLAB
+MATRIX_ROWS = SQUARE_AT + 8 * 256
+SPIN_AT = GY * 2 * 16
+FLOAT_ROWS = SPIN_AT + 256
+
+
+def matrix_pair(matrices, start, which):
+    count = GX * SLAB
+    first = pl.multiple_of(start + which * count, 64)
+    second = pl.multiple_of(start + (which + 2) * count, 64)
+    return matrices[pl.ds(first, count), :], matrices[pl.ds(second, count), :]
+
+
+def square_pair(matrices, which):
+    first = SQUARE_AT + which * 512
+    return matrices[first : first + 256, :], matrices[first + 256 : first + 512, :]
+
+
+def encode(values):
+    largest = jnp.max(jnp.abs(values), axis=1, keepdims=True)
+    scale = (jnp.maximum(largest, 1e-34) * 1.01).astype(BF16).astype(F32)
+    level = values * (2048.0 / scale)
+    second = level * level
+    fourth = second * second
+    eighth = fourth * fourth
+    code = eighth * second * level
+    row = lax.broadcasted_iota(jnp.int32, values.shape, 1)
+    code = jnp.where(row == KX, scale, code)
+    return code.reshape(values.shape[0], SLAB // 8, 8, 128).astype(BF16)
+
+
+def decode(codes):
+    code = codes.astype(F32).reshape(codes.shape[0], SLAB, 128)
+    scale = code[:, KX : KX + 1, :] * (1.0 / 2048.0)
+    level = jnp.exp2(jnp.log2(jnp.abs(code)) * (1.0 / POWER))
+    level = jnp.where(code < 0.0, -level, level)
+    return jnp.where(code == 0.0, 0.0, level) * scale
 
 
 def real_transform(values):
@@ -184,7 +226,7 @@
         wave_x = mode_x.astype(F32) * unit
         wave_y = mode_y.astype(F32) * unit
         square = wave_x * wave_x + wave_y * wave_y
-        scale = 1.0 / (NG * NG)
+        scale = 1.0 / NG
         gain = jnp.where(inside, scale / (1.0 + diffusion * square * square), 0.0)
         stiffness = gravity_step * depth_step * square
         below = 1.0 / (1.0 + coriolis * coriolis + stiffness)
@@ -230,6 +272,7 @@
         return carry
 
     lax.fori_loop(0, KX * (128 // chunk), body, 0)
+    gains[KX] = jnp.zeros((4, 128, 128), F32)
 
 
 def apply_gains(gains, member, real, imag):
@@ -258,10 +301,11 @@
 
 def step_kernel(*refs):
     sources = refs[0:4]
-    (fwd_h, fwd_l, inv_h, inv_l, gat_h, gat_l, sca_h, sca_l, fin_h, fin_l, fout_h, fout_l) = refs[4:16]
-    twist, spin = refs[16:18]
-    results = refs[18:22]
+    matrix_source, float_source = refs[4:6]
+    results = refs[6:10]
     (
+        matrices,
+        floats,
         grid_rows,
         head,
         tail,
@@ -272,6 +316,7 @@
         returned,
         waves,
         new_rows,
+        sem_table,
         sem_rows_out,
         sem_rows_in,
         sem_out,
@@ -280,27 +325,58 @@
         sem_back_in,
         sem_last_out,
         sem_last_in,
-    ) = refs[22:]
+        sem_leaders,
+        sem_all,
+    ) = refs[10:]
     octant = lax.axis_index("gx")
     slot_own = lax.axis_index("gy")
     own = slot_own * GX + octant
+    octants = [(octant + step) % GX for step in range(GX)]
+
+    def slot_at(step):
+        slot = slot_own + step
+        return jnp.where(slot >= GY, slot - GY, slot)
+
+    def slot_before(step):
+        slot = slot_own - step
+        return jnp.where(slot < 0, slot + GY, slot)
 
     barrier = pltpu.get_barrier_semaphore()
-
-    def greet(step, carry):
-        other = (own + step) % DEVICES
+    for step in range(1, GX):
         pl.semaphore_signal(
-            barrier, inc=1, device_id=(other % GX, other // GX), device_id_type=MESH
+            barrier, inc=1, device_id=(octants[step], slot_own), device_id_type=MESH
         )
-        return carry
-
-    lax.fori_loop(1, DEVICES, greet, 0)
-    fill_gains(gains, octant, slot_own)
-    pl.semaphore_wait(barrier, DEVICES - 1)
+
+    @pl.when(octant == 0)
+    def greet_leaders():
+        for step in range(1, GY):
+            pl.semaphore_signal(
+                barrier, inc=1, device_id=(octant, slot_at(step)), device_id_type=MESH
+            )
+
+    table_copies = [
+        pltpu.make_async_copy(matrix_source, matrices, sem_table.at[0]),
+        pltpu.make_async_copy(float_source, floats, sem_table.at[1]),
+    ]
+    for copy in table_copies:
+        copy.start()
+    own_rows = pl.ds(pl.multiple_of(octant * ROWS, ROWS), ROWS)
+    for field in range(FIELDS):
+        pltpu.make_async_copy(
+            sources[field].at[own_rows, :], grid_rows.at[field, octant], sem_rows_in.at[field]
+        ).start()
+
+    @pl.when(octant == 0)
+    def wait_leader():
+        pl.semaphore_wait(barrier, GX - 1 + GY - 1)
+
+    @pl.when(octant != 0)
+    def wait_member():
+        pl.semaphore_wait(barrier, GX - 1)
 
     for field in range(FIELDS):
         for step in range(1, GX):
-            other = (octant + step) % GX
+            other = octants[step]
             pltpu.make_async_remote_copy(
                 src_ref=sources[field].at[pl.ds(pl.multiple_of(other * ROWS, ROWS), ROWS), :],
                 dst_ref=grid_rows.at[field, octant],
@@ -309,11 +385,26 @@
                 device_id=(other, slot_own),
                 device_id_type=MESH,
             ).start()
-        pltpu.make_async_copy(
-            sources[field].at[pl.ds(pl.multiple_of(octant * ROWS, ROWS), ROWS), :],
-            grid_rows.at[field, octant],
-            sem_rows_in.at[field],
-        ).start()
+
+    @pl.when(octant == 0)
+    def tell_leaders():
+        for step in range(1, GY):
+            pl.semaphore_signal(
+                sem_leaders, inc=1, device_id=(octant, slot_at(step)), device_id_type=MESH
+            )
+
+    fill_gains(gains, octant, slot_own)
+
+    @pl.when(octant == 0)
+    def tell_members():
+        pl.semaphore_wait(sem_leaders, GY - 1)
+        for step in range(1, GX):
+            pl.semaphore_signal(
+                sem_all, inc=1, device_id=(octants[step], slot_own), device_id_type=MESH
+            )
+
+    for copy in table_copies:
+        copy.wait()
 
     def row_body(step, carry):
         field = step // 2
@@ -330,7 +421,8 @@
                 real, imag = spectrum[0][0], spectrum[16][0]
             else:
                 wave_real, wave_imag = spectrum[slot]
-                cosine, sine = twist[slot, 0], twist[slot, 1]
+                cosine = floats[32 * slot : 32 * slot + 16, :]
+                sine = floats[32 * slot + 16 : 32 * slot + 32, :]
                 real = wave_real * cosine + wave_imag * sine
                 imag = wave_imag * cosine - wave_real * sine
             for side, value in ((0, real), (128, imag)):
@@ -345,94 +437,131 @@
         ).wait()
         lax.fori_loop(2 * field, 2 * field + 2, row_body, 0)
 
-    def send(place, target, out_sem, in_sem):
+    @pl.when(octant != 0)
+    def wait_all():
+        pl.semaphore_wait(sem_all, 1)
+
+    def send(slot, other, target, out_sem, in_sem):
         pltpu.make_async_remote_copy(
-            src_ref=slabs.at[place],
+            src_ref=slabs.at[slot * GX + other],
             dst_ref=target.at[own],
             send_sem=out_sem,
-            recv_sem=in_sem,
-            device_id=(place % GX, place // GX),
+            recv_sem=in_sem.at[slot_own],
+            device_id=(other, slot),
             device_id_type=MESH,
         ).start()
 
     def slot_product(slot):
-        which = (slot + GY - 1) // GY
+        which = jnp.minimum(slot, 1)
         spectrum = product3(
-            (fwd_h[which], fwd_l[which]), (head[slot], tail[slot]), NT
+            matrix_pair(matrices, FWD_AT, which), (head[slot], tail[slot]), NT
         )
-        slabs[pl.ds(pl.multiple_of(slot * GX, GX), GX)] = spectrum.reshape(GX, SLAB, 128)
+        slabs[pl.ds(slot * GX, GX)] = encode(spectrum.reshape(GX, SLAB, 128))
 
     slot_product(slot_own)
     for step in range(1, GX):
-        send(slot_own * GX + (octant + step) % GX, landed, sem_out, sem_in)
-    pltpu.make_async_copy(slabs.at[own], landed.at[own], sem_in).start()
+        send(slot_own, octants[step], landed, sem_out, sem_in)
+    pltpu.make_async_copy(slabs.at[own], landed.at[own], sem_in.at[slot_own]).start()
 
     def slot_body(step, carry):
-        slot = (slot_own + step) % GY
+        slot = slot_at(step)
         slot_product(slot)
-        for other in range(GX):
-            send(slot * GX + (octant + other) % GX, landed, sem_out, sem_in)
+        for other in octants:
+            send(slot, other, landed, sem_out, sem_in)
         return carry
 
     lax.fori_loop(1, GY, slot_body, 0)
 
-    pltpu.make_async_copy(landed, landed, sem_in).wait()
-
-    def spread(source, carry):
-        columns[pl.ds(source, SLAB, stride=128), :] = landed[source]
-        return carry
-
-    lax.fori_loop(0, DEVICES, spread, 0)
-
-    def column_body(member, carry):
-        real_rows = pl.ds(pl.multiple_of(member * 128, 128), 128)
-        imag_rows = pl.ds(pl.multiple_of((member + SLAB // 2) * 128, 128), 128)
-        values = jnp.concatenate([columns[real_rows, :], columns[imag_rows, :]], axis=0)
-        mixed = product3((gat_h[...], gat_l[...]), parts(values), NN)
-        real, imag = mixed[:128], mixed[128:]
-        cosine, sine = spin[0], spin[1]
-        turned = jnp.concatenate(
-            [real * cosine + imag * sine, imag * cosine - real * sine], axis=1
+    def spread(step, carry):
+        slot = slot_before(step)
+        group = landed.at[pl.ds(slot * GX, GX)]
+        pltpu.make_async_copy(group, group, sem_in.at[slot]).wait()
+        values = decode(landed[pl.ds(slot * GX, GX)])
+        for source in range(GX):
+            columns[pl.ds(slot * GX + source, SLAB, stride=128), :] = values[source]
+        return carry
+
+    lax.fori_loop(0, GY, spread, 0)
+
+    def column_body(pair, carry):
+        real_rows = pl.ds(pl.multiple_of(pair * 256, 256), 256)
+        imag_rows = pl.ds(pl.multiple_of(pair * 256 + SLAB // 2 * 128, 256), 256)
+        real, imag = columns[real_rows, :], columns[imag_rows, :]
+        values = jnp.concatenate(
+            [
+                jnp.concatenate([real[:128], real[128:]], axis=1),
+                jnp.concatenate([imag[:128], imag[128:]], axis=1),
+            ],
+            axis=0,
         )
-        modes = product3(parts(turned), (fin_h[...], fin_l[...]), NN)
-        real, imag = apply_gains(gains, member, modes[:, :128], modes[:, 128:])
-        modes = jnp.concatenate([real, imag], axis=1)
-        mixed = product3(parts(modes), (fout_h[...], fout_l[...]), NN)
-        real, imag = mixed[:, :128], mixed[:, 128:]
+        mixed = product3(square_pair(matrices, 0), parts(values), NN)
+        cosine = floats[SPIN_AT : SPIN_AT + 128, :]
+        sine = floats[SPIN_AT + 128 : SPIN_AT + 256, :]
+        turned = []
+        for side in (0, 128):
+            real, imag = mixed[:128, side : side + 128], mixed[128:, side : side + 128]
+            turned.append(
+                jnp.concatenate([real * cosine + imag * sine, imag * cosine - real * sine], axis=1)
+            )
+        turned = jnp.concatenate(turned, axis=0)
+        modes = product3(parts(turned), square_pair(matrices, 2), NN)
+        changed = []
+        for member in range(2):
+            piece = modes[128 * member : 128 * member + 128]
+            real, imag = apply_gains(gains, 2 * pair + member, piece[:, :128], piece[:, 128:])
+            changed.append(jnp.concatenate([real, imag], axis=1))
+        changed = jnp.concatenate(changed, axis=0)
+        mixed = product3(parts(changed), square_pair(matrices, 3), NN)
+        reals, imags = [], []
+        for member in range(2):
+            piece = mixed[128 * member : 128 * member + 128]
+            real, imag = piece[:, :128], piece[:, 128:]
+            reals.append(real * cosine - imag * sine)
+            imags.append(imag * cosine + real * sine)
         values = jnp.concatenate(
-            [real * cosine - imag * sine, imag * cosine + real * sine], axis=0
+            [jnp.concatenate(reals, axis=1), jnp.concatenate(imags, axis=1)], axis=0
         )
-        values = product3((sca_h[...], sca_l[...]), parts(values), NN)
-        columns[real_rows, :] = values[:128]
-        columns[imag_rows, :] = values[128:]
-        return carry
-
-    lax.fori_loop(0, KX, column_body, 0)
+        values = product3(square_pair(matrices, 1), parts(values), NN)
+        columns[real_rows, :] = jnp.concatenate([values[:128, :128], values[:128, 128:]], axis=0)
+        columns[imag_rows, :] = jnp.concatenate([values[128:, :128], values[128:, 128:]], axis=0)
+        return carry
+
+    lax.fori_loop(0, (KX + 1) // 2, column_body, 0)
 
     sent = slabs.at[pl.ds(0, DEVICES - 1)]
     pltpu.make_async_copy(sent, sent, sem_out).wait()
 
-    def collect(place):
-        slabs[place] = columns[pl.ds(place, SLAB, stride=128), :]
-
-    collect(own)
-    pltpu.make_async_copy(slabs.at[own], returned.at[own], sem_back_in).start()
+    def collect(slot):
+        first = slot * GX
+        values = jnp.stack(
+            [columns[pl.ds(first + source, SLAB, stride=128), :] for source in range(GX)]
+        )
+        slabs[pl.ds(first, GX)] = encode(values)
+
+    collect(slot_own)
+    for step in range(1, GX):
+        send(slot_own, octants[step], returned, sem_back_out, sem_back_in)
+    pltpu.make_async_copy(slabs.at[own], returned.at[own], sem_back_in.at[slot_own]).start()
 
     def back_body(step, carry):
-        place = (own + step) % DEVICES
-        collect(place)
-        send(place, returned, sem_back_out, sem_back_in)
-        return carry
-
-    lax.fori_loop(1, DEVICES, back_body, 0)
-    pltpu.make_async_copy(returned, returned, sem_back_in).wait()
-
-    def wave_body(slot, carry):
-        which = (slot + GY - 1) // GY
-        block = returned[pl.ds(pl.multiple_of(slot * GX, GX), GX)].reshape(GX * SLAB, 128)
-        values = product3(parts(block), (inv_h[which], inv_l[which]), TN)
+        slot = slot_at(step)
+        collect(slot)
+        for other in octants:
+            send(slot, other, returned, sem_back_out, sem_back_in)
+        return carry
+
+    lax.fori_loop(1, GY, back_body, 0)
+
+    def wave_body(step, carry):
+        slot = slot_before(step)
+        group = returned.at[pl.ds(slot * GX, GX)]
+        pltpu.make_async_copy(group, group, sem_back_in.at[slot]).wait()
+        which = jnp.minimum(slot, 1)
+        block = decode(returned[pl.ds(slot * GX, GX)]).reshape(GX * SLAB, 128)
+        values = product3(parts(block), matrix_pair(matrices, INV_AT, which), TN)
         real, imag = values[:, :128], values[:, 128:]
-        cosine, sine = twist[slot, 0, 0:1, :], twist[slot, 1, 0:1, :]
+        cosine = floats[pl.ds(32 * slot, 1), :]
+        sine = floats[pl.ds(32 * slot + 16, 1), :]
         waves[slot, :, 0:128] = real * cosine - imag * sine
         waves[slot, :, 128:256] = imag * cosine + real * sine
         return carry
@@ -455,9 +584,8 @@
 
     for field in range(FIELDS):
         lax.fori_loop(2 * field, 2 * field + 2, grid_body, 0)
-        own_rows = pl.ds(pl.multiple_of(octant * ROWS, ROWS), ROWS)
         for step in range(1, GX):
-            other = (octant + step) % GX
+            other = octants[step]
             pltpu.make_async_remote_copy(
                 src_ref=new_rows.at[field, other],
                 dst_ref=results[field].at[own_rows, :],
@@ -470,7 +598,6 @@
             new_rows.at[field, octant], results[field].at[own_rows, :], sem_last_in.at[field]
         ).start()
 
-    sent = slabs.at[pl.ds(0, DEVICES - 1)]
     pltpu.make_async_copy(sent, sent, sem_back_out).wait()
     for field in range(FIELDS):
         moved = new_rows.at[field, pl.ds(0, GX - 1)]
@@ -482,33 +609,37 @@
 def per_device(east_wind, north_wind, height, tracer):
     constants = [jnp.asarray(value) for value in tables()]
     anywhere = pl.BlockSpec(memory_space=pl.ANY)
-    vmem = pl.BlockSpec(memory_space=pltpu.VMEM)
     block = jax.ShapeDtypeStruct((NG // GY, COLS), BF16)
     dma = pltpu.SemaphoreType.DMA
     return pl.pallas_call(
         step_kernel,
         out_shape=(block,) * 4,
-        in_specs=[anywhere] * 4 + [vmem] * len(constants),
+        in_specs=[anywhere] * 6,
         out_specs=(anywhere,) * 4,
         scratch_shapes=[
+            pltpu.VMEM((MATRIX_ROWS, 256), BF16),
+            pltpu.VMEM((FLOAT_ROWS, 128), F32),
             pltpu.VMEM((FIELDS, GX, ROWS, COLS), BF16),
             pltpu.VMEM((GY, 128, 256), BF16),
             pltpu.VMEM((GY, 128, 256), BF16),
-            pltpu.VMEM((DEVICES, SLAB, 128), F32),
-            pltpu.VMEM((DEVICES, SLAB, 128), F32),
+            pltpu.VMEM((DEVICES, SLAB // 8, 8, 128), BF16),
+            pltpu.VMEM((DEVICES, SLAB // 8, 8, 128), BF16),
             pltpu.VMEM((SLAB * 128, 128), F32),
-            pltpu.VMEM((KX, 4, 128, 128), F32),
-            pltpu.VMEM((DEVICES, SLAB, 128), F32),
+            pltpu.VMEM((KX + 1, 4, 128, 128), F32),
+            pltpu.VMEM((DEVICES, SLAB // 8, 8, 128), BF16),
             pltpu.VMEM((GY, 128, 256), F32),
             pltpu.VMEM((FIELDS, GX, ROWS, COLS), BF16),
+            dma((2,)),
             dma((FIELDS,)),
             dma((FIELDS,)),
             dma,
+            dma((GY,)),
             dma,
-            dma,
-            dma,
+            dma((GY,)),
             dma((FIELDS,)),
             dma((FIELDS,)),
+            pltpu.SemaphoreType.REGULAR,
+            pltpu.SemaphoreType.REGULAR,
         ],
         compiler_params=pltpu.CompilerParams(collective_id=0, has_side_effects=True),
     )(east_wind, north_wind, height, tracer, *constants)

time: 108 us -> 81.3 us (0.75)
  Pallas kernels: 103 us -> 73.8 us
  local copies, waits for them, and re-layouts: 4.5 us -> 6.68 us
    pallas_call x1, Pallas kernels: 103 us -> 73.8 us  [per_device(): pl.pallas_call(step_kernel, out_shape=(block,) * 4, in_specs=[anywhere] *...]
    unnamed x10 -> x4, local copies, waits for them, and re-layouts: 4.5 us -> 6.68 us
where the time goes in v1:
time: 81.3 us; the launch traced here: 81.1 us
  Pallas kernels  73.8 us (91%)
  local copies, waits for them, and re-layouts  6.68 us (8%)
    pallas_call x1, Pallas kernels, per_device(): pl.pallas_call(step_kernel, out_shape=(block,) * 4, in_specs=[anywhere] *...  73.8 us
    unnamed x4, local copies, waits for them, and re-layouts  6.68 us

profile of v1, /device:TPU:1, one launch (start us, length us, event | category | flops | bytes accessed | tf_op | source)
XLA Modules:
  0.0 81.1 jit_solution(16561507356270664437)
XLA Ops:
  0.6 73.8 %shard_map.93 = (bf16[256,512]{1,0:T(8,128)(2,1)}, bf16[256,512]{1,0:T(8,128)(2,1)}, bf16[256,512]{1,0:T(8,128)(2,1)}, bf16[256,512]{1,0:T(8,128)(2,1)}) custom-call(bf16[256,512]{1,0:T(8,128)(2,1)} %refs_0_.1, bf16[256,512]{1,0:T(8,128)(2,1)} %refs_1_.1, bf16[256,512]{1,0:T(8,128)(2,1)} %refs_2_.1, bf16[256,512]{1,0:T(8,128)(2,1)} %refs_3_.1, ...), custom_call_target="tpu_custom_call" | custom-call | tf_op jit(solution)/shard_map/pallas_call | solution.py:614
  74.4 1.7 %copy.14 = bf16[256,512]{1,0:T(8,128)(2,1)} copy(bf16[256,512]{1,0:T(8,128)(2,1)} %get-tuple-element.8) | data formatting | bytes 524288
  76.1 1.7 %copy.15 = bf16[256,512]{1,0:T(8,128)(2,1)} copy(bf16[256,512]{1,0:T(8,128)(2,1)} %get-tuple-element.9) | data formatting | bytes 524288
  77.7 1.7 %copy.16 = bf16[256,512]{1,0:T(8,128)(2,1)} copy(bf16[256,512]{1,0:T(8,128)(2,1)} %get-tuple-element.10) | data formatting | bytes 524288
  79.4 1.7 %copy.17 = bf16[256,512]{1,0:T(8,128)(2,1)} copy(bf16[256,512]{1,0:T(8,128)(2,1)} %get-tuple-element.11) | data formatting | bytes 524288

commit v2 on v1

--- a/solution.py
+++ b/solution.py
@@ -18,6 +18,7 @@
 ROWS = 32
 COLS = 512
 POWER = 11
+UNROLL = 2
 
 coriolis = 0.25
 gravity_step = 2.0
@@ -194,11 +195,9 @@
 def product3(left, right, dims):
     left_head, left_tail = left
     right_head, right_tail = right
-    return (
-        product(left_head, right_head, dims)
-        + product(left_head, right_tail, dims)
-        + product(left_tail, right_head, dims)
-    )
+    left_all = jnp.concatenate([left_head, left_head, left_tail], axis=dims[0][0])
+    right_all = jnp.concatenate([right_head, right_tail, right_head], axis=dims[1][0])
+    return product(left_all, right_all, dims)
 
 
 NN = ((1,), (0,))
@@ -334,12 +333,10 @@
     octants = [(octant + step) % GX for step in range(GX)]
 
     def slot_at(step):
-        slot = slot_own + step
-        return jnp.where(slot >= GY, slot - GY, slot)
+        return (slot_own + 9 * step) % GY
 
     def slot_before(step):
-        slot = slot_own - step
-        return jnp.where(slot < 0, slot + GY, slot)
+        return (slot_own + 16 * GY - 9 * step) % GY
 
     barrier = pltpu.get_barrier_semaphore()
     for step in range(1, GX):
@@ -451,29 +448,36 @@
             device_id_type=MESH,
         ).start()
 
-    def slot_product(slot):
-        which = jnp.minimum(slot, 1)
-        spectrum = product3(
-            matrix_pair(matrices, FWD_AT, which), (head[slot], tail[slot]), NT
-        )
-        slabs[pl.ds(slot * GX, GX)] = encode(spectrum.reshape(GX, SLAB, 128))
-
-    slot_product(slot_own)
+    def slot_products(slots):
+        loaded = [
+            (matrix_pair(matrices, FWD_AT, jnp.minimum(slot, 1)), (head[slot], tail[slot]))
+            for slot in slots
+        ]
+        codes = [
+            encode(product3(left, right, NT).reshape(GX, SLAB, 128)) for left, right in loaded
+        ]
+        for slot, code in zip(slots, codes):
+            slabs[pl.ds(slot * GX, GX)] = code
+
+    def slot_body(step, carry):
+        slots = [slot_at(2 * step + 1), slot_at(2 * step + 2)]
+        slot_products(slots)
+        for slot in slots:
+            for other in octants:
+                send(slot, other, landed, sem_out, sem_in)
+        return carry
+
+    lax.fori_loop(0, GY // 2 - 1, slot_body, 0)
+    far = slot_at(GY - 1)
+    slot_products([far, slot_own])
+    for other in octants:
+        send(far, other, landed, sem_out, sem_in)
     for step in range(1, GX):
         send(slot_own, octants[step], landed, sem_out, sem_in)
     pltpu.make_async_copy(slabs.at[own], landed.at[own], sem_in.at[slot_own]).start()
 
-    def slot_body(step, carry):
-        slot = slot_at(step)
-        slot_product(slot)
-        for other in octants:
-            send(slot, other, landed, sem_out, sem_in)
-        return carry
-
-    lax.fori_loop(1, GY, slot_body, 0)
-
     def spread(step, carry):
-        slot = slot_before(step)
+        slot = slot_before(step + 1)
         group = landed.at[pl.ds(slot * GX, GX)]
         pltpu.make_async_copy(group, group, sem_in.at[slot]).wait()
         values = decode(landed[pl.ds(slot * GX, GX)])
@@ -483,10 +487,12 @@
 
     lax.fori_loop(0, GY, spread, 0)
 
-    def column_body(pair, carry):
+    def row_pairs(pair):
         real_rows = pl.ds(pl.multiple_of(pair * 256, 256), 256)
         imag_rows = pl.ds(pl.multiple_of(pair * 256 + SLAB // 2 * 128, 256), 256)
-        real, imag = columns[real_rows, :], columns[imag_rows, :]
+        return real_rows, imag_rows
+
+    def column_math(pair, real, imag):
         values = jnp.concatenate(
             [
                 jnp.concatenate([real[:128], real[128:]], axis=1),
@@ -522,11 +528,21 @@
             [jnp.concatenate(reals, axis=1), jnp.concatenate(imags, axis=1)], axis=0
         )
         values = product3(square_pair(matrices, 1), parts(values), NN)
-        columns[real_rows, :] = jnp.concatenate([values[:128, :128], values[:128, 128:]], axis=0)
-        columns[imag_rows, :] = jnp.concatenate([values[128:, :128], values[128:, 128:]], axis=0)
-        return carry
-
-    lax.fori_loop(0, (KX + 1) // 2, column_body, 0)
+        return (
+            jnp.concatenate([values[:128, :128], values[:128, 128:]], axis=0),
+            jnp.concatenate([values[128:, :128], values[128:, 128:]], axis=0),
+        )
+
+    def column_body(step, carry):
+        pairs = [UNROLL * step + index for index in range(UNROLL)]
+        loaded = [[columns[rows, :] for rows in row_pairs(pair)] for pair in pairs]
+        done = [column_math(pair, *values) for pair, values in zip(pairs, loaded)]
+        for pair, values in zip(pairs, done):
+            for rows, value in zip(row_pairs(pair), values):
+                columns[rows, :] = value
+        return carry
+
+    lax.fori_loop(0, (KX + 1) // 2 // UNROLL, column_body, 0)
 
     sent = slabs.at[pl.ds(0, DEVICES - 1)]
     pltpu.make_async_copy(sent, sent, sem_out).wait()
@@ -606,15 +622,26 @@
         pltpu.make_async_copy(results[field], results[field], sem_last_in.at[field]).wait()
 
 
+def place_kernel(*refs):
+    copies = [
+        pltpu.make_async_copy(refs[field], refs[FIELDS + field], refs[2 * FIELDS].at[field])
+        for field in range(FIELDS)
+    ]
+    for copy in copies:
+        copy.start()
+    for copy in copies:
+        copy.wait()
+
+
 def per_device(east_wind, north_wind, height, tracer):
     constants = [jnp.asarray(value) for value in tables()]
     anywhere = pl.BlockSpec(memory_space=pl.ANY)
     block = jax.ShapeDtypeStruct((NG // GY, COLS), BF16)
     dma = pltpu.SemaphoreType.DMA
-    return pl.pallas_call(
+    landed = pl.pallas_call(
         step_kernel,
         out_shape=(block,) * 4,
-        in_specs=[anywhere] * 6,
+        in_specs=[pl.BlockSpec(memory_space=pltpu.HBM)] * 6,
         out_specs=(anywhere,) * 4,
         scratch_shapes=[
             pltpu.VMEM((MATRIX_ROWS, 256), BF16),
@@ -641,8 +668,21 @@
             pltpu.SemaphoreType.REGULAR,
             pltpu.SemaphoreType.REGULAR,
         ],
-        compiler_params=pltpu.CompilerParams(collective_id=0, has_side_effects=True),
-    )(east_wind, north_wind, height, tracer, *constants)
+        compiler_params=pltpu.CompilerParams(
+            collective_id=0, has_side_effects=True, vmem_limit_bytes=32 * 1024 * 1024
+        ),
+    )(*[
+        pltpu.with_memory_space_constraint(value, pltpu.HBM)
+        for value in (east_wind, north_wind, height, tracer, *constants)
+    ])
+    return pl.pallas_call(
+        place_kernel,
+        out_shape=(block,) * 4,
+        in_specs=[anywhere] * 4,
+        out_specs=(pl.BlockSpec(memory_space=pltpu.HBM),) * 4,
+        scratch_shapes=[dma((FIELDS,))],
+        compiler_params=pltpu.CompilerParams(vmem_limit_bytes=1024 * 1024),
+    )(*landed)
 
 
 def solution(mesh):

time: 81.3 us -> 71.6 us (0.88)
  local copies, waits for them, and re-layouts: 6.68 us -> 0 us
  Pallas kernels: 73.8 us -> 70.8 us
    unnamed x4 -> x0, local copies, waits for them, and re-layouts: 6.68 us -> none
    pallas_call x1 -> x2, Pallas kernels: 73.8 us -> 70.8 us  [the longest x1 69.8 us: per_device(): pl.pallas_call(step_kernel, out_shape=(block,) * 4, in_specs=[pl.BlockSpe...]
where the time goes in v2:
time: 71.6 us; the launch traced here: 71.5 us
  Pallas kernels  70.8 us (99%)
    pallas_call x1, Pallas kernels, per_device(): pl.pallas_call(step_kernel, out_shape=(block,) * 4, in_specs=[pl.BlockSpe...  69.8 us

profile of v2, /device:TPU:1, one launch (start us, length us, event | category | flops | bytes accessed | tf_op | source)
XLA Modules:
  0.0 71.5 jit_solution(18069584059341941633)
XLA Ops:
  0.6 69.8 %shard_map.93 = (bf16[256,512]{1,0:T(8,128)(2,1)S(1)}, bf16[256,512]{1,0:T(8,128)(2,1)S(1)}, bf16[256,512]{1,0:T(8,128)(2,1)S(1)}, bf16[256,512]{1,0:T(8,128)(2,1)S(1)}) custom-call(bf16[256,512]{1,0:T(8,128)(2,1)} %refs_0_.1, bf16[256,512]{1,0:T(8,128)(2,1)} %refs_1_.1, bf16[256,512]{1,0:T(8,128)(2,1)} %refs_2_.1, bf16[256,512]{1,0:T(8,128)(2,1)} %refs_3_.1, ...), custom_call_target="tpu_custom_call" | custom-call | tf_op jit(solution)/shard_map/pallas_call | solution.py:641
  70.5 1.0 %shard_map.94 = (bf16[256,512]{1,0:T(8,128)(2,1)}, bf16[256,512]{1,0:T(8,128)(2,1)}, bf16[256,512]{1,0:T(8,128)(2,1)}, bf16[256,512]{1,0:T(8,128)(2,1)}) custom-call(bf16[256,512]{1,0:T(8,128)(2,1)S(1)} %get-tuple-element.8.refs_0_, bf16[256,512]{1,0:T(8,128)(2,1)S(1)} %get-tuple-element.9.refs_1_, bf16[256,512]{1,0:T(8,128)(2,1)S(1)} %get-tuple-element.10.refs_2_, ...), custom_call_target="tpu_custom_call" | custom-call | tf_op jit(solution)/shard_map/pallas_call | solution.py:678

commit v3 on v2

--- a/solution.py
+++ b/solution.py
@@ -15,10 +15,13 @@
 DEVICES = GX * GY
 KX = 11
 SLAB = 24
+FIRST = 16
+PLANE = 136
+REAL_ROWS = (0, 1, 2, 3, 4, 5, 6, 7, 17, 18, 19)
+IMAG_ROWS = (8, 9, 10, 11, 12, 13, 14, 16, 20, 21, 22)
 ROWS = 32
 COLS = 512
 POWER = 11
-UNROLL = 2
 
 coriolis = 0.25
 gravity_step = 2.0
@@ -47,24 +50,25 @@
 def tables():
     turn = 2.0 * np.pi
     lane = np.arange(128)
-    forward = np.zeros((2, GX, 2, SLAB // 2, 256))
-    inverse = np.zeros((2, GX, 2, SLAB // 2, 256))
+    forward = np.zeros((2, GX, SLAB, 256))
+    inverse = np.zeros((2, GX, SLAB, 256))
     for place in range(86):
         octant, member = place // KX, place % KX
+        real_row, imag_row = REAL_ROWS[member], IMAG_ROWS[member]
         low = place - 43
         cosine, sine = np.cos(turn * lane * low / 128), np.sin(turn * lane * low / 128)
-        forward[1, octant, 0, member] = np.concatenate([cosine, sine])
-        forward[1, octant, 1, member] = np.concatenate([-sine, cosine])
-        inverse[1, octant, 0, member] = np.concatenate([cosine, sine])
-        inverse[1, octant, 1, member] = np.concatenate([-sine, cosine])
+        forward[1, octant, real_row] = np.concatenate([cosine, sine])
+        forward[1, octant, imag_row] = np.concatenate([-sine, cosine])
+        inverse[1, octant, real_row] = np.concatenate([cosine, sine])
+        inverse[1, octant, imag_row] = np.concatenate([-sine, cosine])
         wave = wave_of(0, place)
         cosine, sine = np.cos(turn * lane * wave / NG), np.sin(turn * lane * wave / NG)
         half = 0 if place < 43 else 128
         weight = 1.0 if wave == 0 else 2.0
-        forward[0, octant, 0, member, half : half + 128] = cosine
-        forward[0, octant, 1, member, half : half + 128] = -sine
-        inverse[0, octant, 0, member, half : half + 128] = weight * cosine
-        inverse[0, octant, 1, member, half : half + 128] = -weight * sine
+        forward[0, octant, real_row, half : half + 128] = cosine
+        forward[0, octant, imag_row, half : half + 128] = -sine
+        inverse[0, octant, real_row, half : half + 128] = weight * cosine
+        inverse[0, octant, imag_row, half : half + 128] = -weight * sine
     forward = forward.reshape(2, GX * SLAB, 256)
     inverse = inverse.reshape(2, GX * SLAB, 256)
     angle = turn * np.outer(np.arange(GY), lane) / NG
@@ -108,21 +112,23 @@
 
 
 def encode(values):
+    rows = values.shape[1]
+    last = lax.broadcasted_iota(jnp.int32, values.shape, 1) == rows - 1
+    values = jnp.where(last, 0.0, values)
     largest = jnp.max(jnp.abs(values), axis=1, keepdims=True)
     scale = (jnp.maximum(largest, 1e-34) * 1.01).astype(BF16).astype(F32)
     level = values * (2048.0 / scale)
     second = level * level
     fourth = second * second
     eighth = fourth * fourth
-    code = eighth * second * level
-    row = lax.broadcasted_iota(jnp.int32, values.shape, 1)
-    code = jnp.where(row == KX, scale, code)
-    return code.reshape(values.shape[0], SLAB // 8, 8, 128).astype(BF16)
+    code = jnp.where(last, scale, eighth * second * level)
+    return code.reshape(values.shape[0], rows // 8, 8, 128).astype(BF16)
 
 
 def decode(codes):
-    code = codes.astype(F32).reshape(codes.shape[0], SLAB, 128)
-    scale = code[:, KX : KX + 1, :] * (1.0 / 2048.0)
+    rows = codes.shape[1] * 8
+    code = codes.astype(F32).reshape(codes.shape[0], rows, 128)
+    scale = code[:, rows - 1 : rows, :] * (1.0 / 2048.0)
     level = jnp.exp2(jnp.log2(jnp.abs(code)) * (1.0 / POWER))
     level = jnp.where(code < 0.0, -level, level)
     return jnp.where(code == 0.0, 0.0, level) * scale
@@ -271,7 +277,6 @@
         return carry
 
     lax.fori_loop(0, KX * (128 // chunk), body, 0)
-    gains[KX] = jnp.zeros((4, 128, 128), F32)
 
 
 def apply_gains(gains, member, real, imag):
@@ -330,25 +335,40 @@
     octant = lax.axis_index("gx")
     slot_own = lax.axis_index("gy")
     own = slot_own * GX + octant
-    octants = [(octant + step) % GX for step in range(GX)]
-
-    def slot_at(step):
-        return (slot_own + 9 * step) % GY
-
-    def slot_before(step):
-        return (slot_own + 16 * GY - 9 * step) % GY
+    octants = [
+        4 * ((octant // 4 + across) % 2) + (octant % 4 + along) % 4
+        for across, along in ((1, 2), (1, 1), (1, 3), (0, 2), (1, 0), (0, 1), (0, 3), (0, 0))
+    ]
+    half_own = slot_own // 8
+    level_own = (slot_own // 2) % 4
+    core_own = slot_own % 2
+
+    def distance(step):
+        turn = step % 4
+        level = jnp.where(turn == 3, 0, jnp.where(turn == 2, 3, 2 - turn))
+        return 1 - step // 4, level
+
+    def slots_at(step):
+        half, level = distance(step)
+        base = 8 * ((half_own + half) % 2) + 2 * ((level_own + level) % 4)
+        return [base + 1 - core_own, base + core_own]
+
+    def slots_before(step):
+        half, level = distance(GY // 2 - 1 - step)
+        base = 8 * ((half_own + half) % 2) + 2 * ((level_own + 4 - level) % 4)
+        return [base + 1 - core_own, base + core_own]
 
     barrier = pltpu.get_barrier_semaphore()
-    for step in range(1, GX):
+    for other in octants[:-1]:
         pl.semaphore_signal(
-            barrier, inc=1, device_id=(octants[step], slot_own), device_id_type=MESH
+            barrier, inc=1, device_id=(other, slot_own), device_id_type=MESH
         )
 
     @pl.when(octant == 0)
     def greet_leaders():
         for step in range(1, GY):
             pl.semaphore_signal(
-                barrier, inc=1, device_id=(octant, slot_at(step)), device_id_type=MESH
+                barrier, inc=1, device_id=(octant, (slot_own + step) % GY), device_id_type=MESH
             )
 
     table_copies = [
@@ -372,8 +392,7 @@
         pl.semaphore_wait(barrier, GX - 1)
 
     for field in range(FIELDS):
-        for step in range(1, GX):
-            other = octants[step]
+        for other in octants[:-1]:
             pltpu.make_async_remote_copy(
                 src_ref=sources[field].at[pl.ds(pl.multiple_of(other * ROWS, ROWS), ROWS), :],
                 dst_ref=grid_rows.at[field, octant],
@@ -387,7 +406,7 @@
     def tell_leaders():
         for step in range(1, GY):
             pl.semaphore_signal(
-                sem_leaders, inc=1, device_id=(octant, slot_at(step)), device_id_type=MESH
+                sem_leaders, inc=1, device_id=(octant, (slot_own + step) % GY), device_id_type=MESH
             )
 
     fill_gains(gains, octant, slot_own)
@@ -395,9 +414,9 @@
     @pl.when(octant == 0)
     def tell_members():
         pl.semaphore_wait(sem_leaders, GY - 1)
-        for step in range(1, GX):
+        for other in octants[:-1]:
             pl.semaphore_signal(
-                sem_all, inc=1, device_id=(octants[step], slot_own), device_id_type=MESH
+                sem_all, inc=1, device_id=(other, slot_own), device_id_type=MESH
             )
 
     for copy in table_copies:
@@ -438,89 +457,118 @@
     def wait_all():
         pl.semaphore_wait(sem_all, 1)
 
-    def send(slot, other, target, out_sem, in_sem):
-        pltpu.make_async_remote_copy(
-            src_ref=slabs.at[slot * GX + other],
-            dst_ref=target.at[own],
-            send_sem=out_sem,
-            recv_sem=in_sem.at[slot_own],
-            device_id=(other, slot),
-            device_id_type=MESH,
+    sides = (pl.ds(0, FIRST // 8), pl.ds(FIRST // 8, (SLAB - FIRST) // 8))
+
+    def send_slot(side, slot, others, target, out_sem, in_sem):
+        for other in others:
+            pltpu.make_async_remote_copy(
+                src_ref=slabs.at[slot * GX + other, sides[side]],
+                dst_ref=target.at[own, sides[side]],
+                send_sem=out_sem.at[side],
+                recv_sem=in_sem.at[side, slot_own],
+                device_id=(other, slot),
+                device_id_type=MESH,
+            ).start()
+
+    def keep_own(side, target, in_sem):
+        pltpu.make_async_copy(
+            slabs.at[own, sides[side]], target.at[own, sides[side]], in_sem.at[side, slot_own]
         ).start()
+
+    def wait_group(side, slot, target, in_sem):
+        group = target.at[pl.ds(slot * GX, GX), sides[side]]
+        pltpu.make_async_copy(group, group, in_sem.at[side, slot]).wait()
+
+    def wait_sent(side, out_sem):
+        sent = slabs.at[pl.ds(0, DEVICES - 1), sides[side]]
+        pltpu.make_async_copy(sent, sent, out_sem.at[side]).wait()
 
     def slot_products(slots):
         loaded = [
             (matrix_pair(matrices, FWD_AT, jnp.minimum(slot, 1)), (head[slot], tail[slot]))
             for slot in slots
         ]
-        codes = [
-            encode(product3(left, right, NT).reshape(GX, SLAB, 128)) for left, right in loaded
-        ]
-        for slot, code in zip(slots, codes):
-            slabs[pl.ds(slot * GX, GX)] = code
+        codes = []
+        for left, right in loaded:
+            spectrum = product3(left, right, NT).reshape(GX, SLAB, 128)
+            codes.append([encode(spectrum[:, :FIRST]), encode(spectrum[:, FIRST:])])
+        for slot, pieces in zip(slots, codes):
+            for side in range(2):
+                slabs[pl.ds(slot * GX, GX), sides[side]] = pieces[side]
+
+    steps = GY // 2
 
     def slot_body(step, carry):
-        slots = [slot_at(2 * step + 1), slot_at(2 * step + 2)]
+        slots = slots_at(step)
         slot_products(slots)
         for slot in slots:
-            for other in octants:
-                send(slot, other, landed, sem_out, sem_in)
+            send_slot(0, slot, octants, landed, sem_out, sem_in)
         return carry
 
-    lax.fori_loop(0, GY // 2 - 1, slot_body, 0)
-    far = slot_at(GY - 1)
-    slot_products([far, slot_own])
-    for other in octants:
-        send(far, other, landed, sem_out, sem_in)
-    for step in range(1, GX):
-        send(slot_own, octants[step], landed, sem_out, sem_in)
-    pltpu.make_async_copy(slabs.at[own], landed.at[own], sem_in.at[slot_own]).start()
-
-    def spread(step, carry):
-        slot = slot_before(step + 1)
-        group = landed.at[pl.ds(slot * GX, GX)]
-        pltpu.make_async_copy(group, group, sem_in.at[slot]).wait()
-        values = decode(landed[pl.ds(slot * GX, GX)])
-        for source in range(GX):
-            columns[pl.ds(slot * GX + source, SLAB, stride=128), :] = values[source]
+    lax.fori_loop(0, steps - 1, slot_body, 0)
+    twin = slots_at(steps - 1)[0]
+    slot_products([twin, slot_own])
+    send_slot(0, twin, octants, landed, sem_out, sem_in)
+    send_slot(0, slot_own, octants[:-1], landed, sem_out, sem_in)
+    keep_own(0, landed, sem_in)
+
+    def second_body(step, carry):
+        for slot in slots_at(step):
+            send_slot(1, slot, octants, landed, sem_out, sem_in)
         return carry
 
-    lax.fori_loop(0, GY, spread, 0)
-
-    def row_pairs(pair):
-        real_rows = pl.ds(pl.multiple_of(pair * 256, 256), 256)
-        imag_rows = pl.ds(pl.multiple_of(pair * 256 + SLAB // 2 * 128, 256), 256)
-        return real_rows, imag_rows
-
-    def column_math(pair, real, imag):
+    lax.fori_loop(0, steps - 1, second_body, 0)
+    send_slot(1, twin, octants, landed, sem_out, sem_in)
+    send_slot(1, slot_own, octants[:-1], landed, sem_out, sem_in)
+    keep_own(1, landed, sem_in)
+
+    def spread(side):
+        first = 0 if side == 0 else FIRST
+        count = FIRST if side == 0 else SLAB - FIRST
+
+        def body(step, carry):
+            for slot in slots_before(step):
+                wait_group(side, slot, landed, sem_in)
+                values = decode(landed[pl.ds(slot * GX, GX), sides[side]])
+                for source in range(GX):
+                    columns[
+                        pl.ds(first * PLANE + slot * GX + source, count, stride=PLANE), :
+                    ] = values[source]
+            return carry
+
+        return body
+
+    def plane(row):
+        return slice(row * 128, row * 128 + 128)
+
+    def column_rows(row):
+        return slice(row * PLANE, row * PLANE + 128)
+
+    def column_math(members, reals, imags):
         values = jnp.concatenate(
-            [
-                jnp.concatenate([real[:128], real[128:]], axis=1),
-                jnp.concatenate([imag[:128], imag[128:]], axis=1),
-            ],
-            axis=0,
+            [jnp.concatenate(reals, axis=1), jnp.concatenate(imags, axis=1)], axis=0
         )
         mixed = product3(square_pair(matrices, 0), parts(values), NN)
         cosine = floats[SPIN_AT : SPIN_AT + 128, :]
         sine = floats[SPIN_AT + 128 : SPIN_AT + 256, :]
         turned = []
-        for side in (0, 128):
-            real, imag = mixed[:128, side : side + 128], mixed[128:, side : side + 128]
+        for index in range(len(members)):
+            real, imag = mixed[:128, plane(index)], mixed[128:, plane(index)]
             turned.append(
                 jnp.concatenate([real * cosine + imag * sine, imag * cosine - real * sine], axis=1)
             )
         turned = jnp.concatenate(turned, axis=0)
         modes = product3(parts(turned), square_pair(matrices, 2), NN)
         changed = []
-        for member in range(2):
-            piece = modes[128 * member : 128 * member + 128]
-            real, imag = apply_gains(gains, 2 * pair + member, piece[:, :128], piece[:, 128:])
+        for index, member in enumerate(members):
+            piece = modes[plane(index)]
+            real, imag = apply_gains(gains, member, piece[:, :128], piece[:, 128:])
             changed.append(jnp.concatenate([real, imag], axis=1))
         changed = jnp.concatenate(changed, axis=0)
         mixed = product3(parts(changed), square_pair(matrices, 3), NN)
         reals, imags = [], []
-        for member in range(2):
-            piece = mixed[128 * member : 128 * member + 128]
+        for index in range(len(members)):
+            piece = mixed[plane(index)]
             real, imag = piece[:, :128], piece[:, 128:]
             reals.append(real * cosine - imag * sine)
             imags.append(imag * cosine + real * sine)
@@ -528,61 +576,86 @@
             [jnp.concatenate(reals, axis=1), jnp.concatenate(imags, axis=1)], axis=0
         )
         values = product3(square_pair(matrices, 1), parts(values), NN)
-        return (
-            jnp.concatenate([values[:128, :128], values[:128, 128:]], axis=0),
-            jnp.concatenate([values[128:, :128], values[128:, 128:]], axis=0),
+        return [
+            (values[:128, plane(index)], values[128:, plane(index)])
+            for index in range(len(members))
+        ]
+
+    def work_columns(groups):
+        loaded = [
+            [
+                [columns[column_rows(rows[member]), :] for member in group]
+                for rows in (REAL_ROWS, IMAG_ROWS)
+            ]
+            for group in groups
+        ]
+        done = [column_math(group, *values) for group, values in zip(groups, loaded)]
+        for group, results_of in zip(groups, done):
+            for member, (real, imag) in zip(group, results_of):
+                columns[column_rows(REAL_ROWS[member]), :] = real
+                columns[column_rows(IMAG_ROWS[member]), :] = imag
+
+    def collect(side, slot):
+        first = 0 if side == 0 else FIRST
+        count = FIRST if side == 0 else SLAB - FIRST
+        values = jnp.stack(
+            [
+                columns[pl.ds(first * PLANE + slot * GX + source, count, stride=PLANE), :]
+                for source in range(GX)
+            ]
         )
-
-    def column_body(step, carry):
-        pairs = [UNROLL * step + index for index in range(UNROLL)]
-        loaded = [[columns[rows, :] for rows in row_pairs(pair)] for pair in pairs]
-        done = [column_math(pair, *values) for pair, values in zip(pairs, loaded)]
-        for pair, values in zip(pairs, done):
-            for rows, value in zip(row_pairs(pair), values):
-                columns[rows, :] = value
+        slabs[pl.ds(slot * GX, GX), sides[side]] = encode(values)
+
+    def send_back(side):
+        def body(step, carry):
+            slots = slots_at(step)
+            for slot in slots:
+                collect(side, slot)
+                send_slot(side, slot, octants, returned, sem_back_out, sem_back_in)
+            return carry
+
+        wait_sent(side, sem_out)
+        lax.fori_loop(0, steps - 1, body, 0)
+        collect(side, twin)
+        send_slot(side, twin, octants, returned, sem_back_out, sem_back_in)
+        collect(side, slot_own)
+        send_slot(side, slot_own, octants[:-1], returned, sem_back_out, sem_back_in)
+        keep_own(side, returned, sem_back_in)
+
+    lax.fori_loop(0, steps, spread(0), 0)
+    work_columns([(0, 1), (2, 3), (4, 5)])
+    lax.fori_loop(0, steps, spread(1), 0)
+    work_columns([(6, 7)])
+    send_back(0)
+    work_columns([(8, 9), (10,)])
+    send_back(1)
+
+    def wave_body(step, carry):
+        slots = slots_before(step)
+        for side in range(2):
+            for slot in slots:
+                wait_group(side, slot, returned, sem_back_in)
+        loaded = [
+            (
+                [returned[pl.ds(slot * GX, GX), sides[side]] for side in range(2)],
+                matrix_pair(matrices, INV_AT, jnp.minimum(slot, 1)),
+                floats[pl.ds(32 * slot, 1), :],
+                floats[pl.ds(32 * slot + 16, 1), :],
+            )
+            for slot in slots
+        ]
+        done = []
+        for codes, right, cosine, sine in loaded:
+            block = jnp.concatenate([decode(code) for code in codes], axis=1)
+            values = product3(parts(block.reshape(GX * SLAB, 128)), right, TN)
+            real, imag = values[:, :128], values[:, 128:]
+            done.append((real * cosine - imag * sine, imag * cosine + real * sine))
+        for slot, (real, imag) in zip(slots, done):
+            waves[slot, :, 0:128] = real
+            waves[slot, :, 128:256] = imag
         return carry
 
-    lax.fori_loop(0, (KX + 1) // 2 // UNROLL, column_body, 0)
-
-    sent = slabs.at[pl.ds(0, DEVICES - 1)]
-    pltpu.make_async_copy(sent, sent, sem_out).wait()
-
-    def collect(slot):
-        first = slot * GX
-        values = jnp.stack(
-            [columns[pl.ds(first + source, SLAB, stride=128), :] for source in range(GX)]
-        )
-        slabs[pl.ds(first, GX)] = encode(values)
-
-    collect(slot_own)
-    for step in range(1, GX):
-        send(slot_own, octants[step], returned, sem_back_out, sem_back_in)
-    pltpu.make_async_copy(slabs.at[own], returned.at[own], sem_back_in.at[slot_own]).start()
-
-    def back_body(step, carry):
-        slot = slot_at(step)
-        collect(slot)
-        for other in octants:
-            send(slot, other, returned, sem_back_out, sem_back_in)
-        return carry
-
-    lax.fori_loop(1, GY, back_body, 0)
-
-    def wave_body(step, carry):
-        slot = slot_before(step)
-        group = returned.at[pl.ds(slot * GX, GX)]
-        pltpu.make_async_copy(group, group, sem_back_in.at[slot]).wait()
-        which = jnp.minimum(slot, 1)
-        block = decode(returned[pl.ds(slot * GX, GX)]).reshape(GX * SLAB, 128)
-        values = product3(parts(block), matrix_pair(matrices, INV_AT, which), TN)
-        real, imag = values[:, :128], values[:, 128:]
-        cosine = floats[pl.ds(32 * slot, 1), :]
-        sine = floats[pl.ds(32 * slot + 16, 1), :]
-        waves[slot, :, 0:128] = real * cosine - imag * sine
-        waves[slot, :, 128:256] = imag * cosine + real * sine
-        return carry
-
-    lax.fori_loop(0, GY, wave_body, 0)
+    lax.fori_loop(0, steps, wave_body, 0)
 
     def grid_body(step, carry):
         field = step // 2
@@ -600,8 +673,7 @@
 
     for field in range(FIELDS):
         lax.fori_loop(2 * field, 2 * field + 2, grid_body, 0)
-        for step in range(1, GX):
-            other = octants[step]
+        for other in octants[:-1]:
             pltpu.make_async_remote_copy(
                 src_ref=new_rows.at[field, other],
                 dst_ref=results[field].at[own_rows, :],
@@ -614,7 +686,8 @@
             new_rows.at[field, octant], results[field].at[own_rows, :], sem_last_in.at[field]
         ).start()
 
-    pltpu.make_async_copy(sent, sent, sem_back_out).wait()
+    for side in range(2):
+        wait_sent(side, sem_back_out)
     for field in range(FIELDS):
         moved = new_rows.at[field, pl.ds(0, GX - 1)]
         pltpu.make_async_copy(moved, moved, sem_rows_out.at[field]).wait()
@@ -651,18 +724,18 @@
             pltpu.VMEM((GY, 128, 256), BF16),
             pltpu.VMEM((DEVICES, SLAB // 8, 8, 128), BF16),
             pltpu.VMEM((DEVICES, SLAB // 8, 8, 128), BF16),
-            pltpu.VMEM((SLAB * 128, 128), F32),
-            pltpu.VMEM((KX + 1, 4, 128, 128), F32),
+            pltpu.VMEM((SLAB * PLANE, 128), F32),
+            pltpu.VMEM((KX, 4, 128, 128), F32),
             pltpu.VMEM((DEVICES, SLAB // 8, 8, 128), BF16),
             pltpu.VMEM((GY, 128, 256), F32),
             pltpu.VMEM((FIELDS, GX, ROWS, COLS), BF16),
             dma((2,)),
             dma((FIELDS,)),
             dma((FIELDS,)),
-            dma,
-            dma((GY,)),
-            dma,
-            dma((GY,)),
+            dma((2,)),
+            dma((2, GY)),
+            dma((2,)),
+            dma((2, GY)),
             dma((FIELDS,)),
             dma((FIELDS,)),
             pltpu.SemaphoreType.REGULAR,

time: 71.6 us -> 69.9 us (0.976)
  Pallas kernels: 70.8 us -> 69.1 us
    pallas_call x1, Pallas kernels: 69.8 us -> 68.1 us  [per_device(): pl.pallas_call(step_kernel, out_shape=(block,) * 4, in_specs=[pl.BlockSpe...]
where the time goes in v3:
time: 69.9 us; the launch traced here: 69.8 us
  Pallas kernels  69.1 us (99%)
    pallas_call x1, Pallas kernels, per_device(): pl.pallas_call(step_kernel, out_shape=(block,) * 4, in_specs=[pl.BlockSpe...  68.1 us

profile of v3, /device:TPU:1, one launch (start us, length us, event | category | flops | bytes accessed | tf_op | source)
XLA Modules:
  0.0 69.8 jit_solution(17540179459621622606)
XLA Ops:
  0.6 68.1 %shard_map.93 = (bf16[256,512]{1,0:T(8,128)(2,1)S(1)}, bf16[256,512]{1,0:T(8,128)(2,1)S(1)}, bf16[256,512]{1,0:T(8,128)(2,1)S(1)}, bf16[256,512]{1,0:T(8,128)(2,1)S(1)}) custom-call(bf16[256,512]{1,0:T(8,128)(2,1)} %refs_0_.1, bf16[256,512]{1,0:T(8,128)(2,1)} %refs_1_.1, bf16[256,512]{1,0:T(8,128)(2,1)} %refs_2_.1, bf16[256,512]{1,0:T(8,128)(2,1)} %refs_3_.1, ...), custom_call_target="tpu_custom_call" | custom-call | tf_op jit(solution)/shard_map/pallas_call | solution.py:714
  68.8 1.0 %shard_map.94 = (bf16[256,512]{1,0:T(8,128)(2,1)}, bf16[256,512]{1,0:T(8,128)(2,1)}, bf16[256,512]{1,0:T(8,128)(2,1)}, bf16[256,512]{1,0:T(8,128)(2,1)}) custom-call(bf16[256,512]{1,0:T(8,128)(2,1)S(1)} %get-tuple-element.8.refs_0_, bf16[256,512]{1,0:T(8,128)(2,1)S(1)} %get-tuple-element.9.refs_1_, bf16[256,512]{1,0:T(8,128)(2,1)S(1)} %get-tuple-element.10.refs_2_, ...), custom_call_target="tpu_custom_call" | custom-call | tf_op jit(solution)/shard_map/pallas_call | solution.py:751

commit v4 on v3

--- a/solution.py
+++ b/solution.py
@@ -70,7 +70,13 @@
         inverse[0, octant, real_row, half : half + 128] = weight * cosine
         inverse[0, octant, imag_row, half : half + 128] = -weight * sine
     forward = forward.reshape(2, GX * SLAB, 256)
-    inverse = inverse.reshape(2, GX * SLAB, 256)
+    inverse = np.concatenate(
+        [
+            inverse[:, :, :FIRST].reshape(2, GX * FIRST, 256),
+            inverse[:, :, FIRST:].reshape(2, GX * (SLAB - FIRST), 256),
+        ],
+        axis=1,
+    )
     angle = turn * np.outer(np.arange(GY), lane) / NG
     twist = np.stack([np.cos(angle), np.sin(angle)], axis=1)[:, :, None, :]
     twist = np.broadcast_to(twist, (GY, 2, 16, 128)).astype(np.float32)
@@ -99,10 +105,9 @@
 FLOAT_ROWS = SPIN_AT + 256
 
 
-def matrix_pair(matrices, start, which):
-    count = GX * SLAB
-    first = pl.multiple_of(start + which * count, 64)
-    second = pl.multiple_of(start + (which + 2) * count, 64)
+def matrix_pair(matrices, start, which, count=GX * SLAB):
+    first = pl.multiple_of(start + which * (GX * SLAB), 64)
+    second = pl.multiple_of(start + (which + 2) * (GX * SLAB), 64)
     return matrices[pl.ds(first, count), :], matrices[pl.ds(second, count), :]
 
 
@@ -113,15 +118,17 @@
 
 def encode(values):
     rows = values.shape[1]
-    last = lax.broadcasted_iota(jnp.int32, values.shape, 1) == rows - 1
-    values = jnp.where(last, 0.0, values)
     largest = jnp.max(jnp.abs(values), axis=1, keepdims=True)
     scale = (jnp.maximum(largest, 1e-34) * 1.01).astype(BF16).astype(F32)
     level = values * (2048.0 / scale)
     second = level * level
     fourth = second * second
     eighth = fourth * fourth
-    code = jnp.where(last, scale, eighth * second * level)
+    code = eighth * second * level
+    ending = code[:, rows - 8 :]
+    last = lax.broadcasted_iota(jnp.int32, ending.shape, 1) == 7
+    ending = jnp.where(last, scale, ending)
+    code = jnp.concatenate([code[:, : rows - 8], ending], axis=1) if rows > 8 else ending
     return code.reshape(values.shape[0], rows // 8, 8, 128).astype(BF16)
 
 
@@ -129,9 +136,8 @@
     rows = codes.shape[1] * 8
     code = codes.astype(F32).reshape(codes.shape[0], rows, 128)
     scale = code[:, rows - 1 : rows, :] * (1.0 / 2048.0)
-    level = jnp.exp2(jnp.log2(jnp.abs(code)) * (1.0 / POWER))
-    level = jnp.where(code < 0.0, -level, level)
-    return jnp.where(code == 0.0, 0.0, level) * scale
+    size = jnp.maximum(jnp.abs(code), 2.0**-126)
+    return jnp.exp2(jnp.log2(size) * (1.0 / POWER - 1.0)) * (code * scale)
 
 
 def real_transform(values):
@@ -344,9 +350,11 @@
     core_own = slot_own % 2
 
     def distance(step):
-        turn = step % 4
-        level = jnp.where(turn == 3, 0, jnp.where(turn == 2, 3, 2 - turn))
-        return 1 - step // 4, level
+        turn = step // 2
+        odd = step % 2
+        far = jnp.where(turn == 3, 0, jnp.where(turn == 2, 3, 2 - turn))
+        near = jnp.where(turn == 3, 0, turn + 1)
+        return 1 - odd, jnp.where(odd == 1, near, far)
 
     def slots_at(step):
         half, level = distance(step)
@@ -354,15 +362,20 @@
         return [base + 1 - core_own, base + core_own]
 
     def slots_before(step):
-        half, level = distance(GY // 2 - 1 - step)
+        half, level = distance(step)
         base = 8 * ((half_own + half) % 2) + 2 * ((level_own + 4 - level) % 4)
         return [base + 1 - core_own, base + core_own]
 
     barrier = pltpu.get_barrier_semaphore()
-    for other in octants[:-1]:
-        pl.semaphore_signal(
-            barrier, inc=1, device_id=(other, slot_own), device_id_type=MESH
-        )
+    across_own = octant // 4
+    for across, along in ((0, 1), (0, 2), (0, 3), (1, 0), (1, 1), (1, 2), (1, 3)):
+        other = 4 * ((across_own + across) % 2) + (octant % 4 + along) % 4
+
+        @pl.when(other != 0)
+        def greet_member():
+            pl.semaphore_signal(
+                barrier, inc=1, device_id=(other, slot_own), device_id_type=MESH
+            )
 
     @pl.when(octant == 0)
     def greet_leaders():
@@ -383,13 +396,19 @@
             sources[field].at[own_rows, :], grid_rows.at[field, octant], sem_rows_in.at[field]
         ).start()
 
-    @pl.when(octant == 0)
-    def wait_leader():
-        pl.semaphore_wait(barrier, GX - 1 + GY - 1)
-
     @pl.when(octant != 0)
     def wait_member():
         pl.semaphore_wait(barrier, GX - 1)
+
+    @pl.when(octant == 1)
+    def release_leader():
+        pl.semaphore_signal(
+            sem_all, inc=1, device_id=(octant - 1, slot_own), device_id_type=MESH
+        )
+
+    @pl.when(octant == 0)
+    def wait_release():
+        pl.semaphore_wait(sem_all, 1)
 
     for field in range(FIELDS):
         for other in octants[:-1]:
@@ -402,17 +421,18 @@
                 device_id_type=MESH,
             ).start()
 
+    fill_gains(gains, octant, slot_own)
+
     @pl.when(octant == 0)
-    def tell_leaders():
+    def tell_members():
+        pl.semaphore_wait(barrier, GY - 1)
         for step in range(1, GY):
             pl.semaphore_signal(
-                sem_leaders, inc=1, device_id=(octant, (slot_own + step) % GY), device_id_type=MESH
+                sem_leaders,
+                inc=1,
+                device_id=(octant, (slot_own + step) % GY),
+                device_id_type=MESH,
             )
-
-    fill_gains(gains, octant, slot_own)
-
-    @pl.when(octant == 0)
-    def tell_members():
         pl.semaphore_wait(sem_leaders, GY - 1)
         for other in octants[:-1]:
             pl.semaphore_signal(
@@ -544,56 +564,60 @@
     def column_rows(row):
         return slice(row * PLANE, row * PLANE + 128)
 
-    def column_math(members, reals, imags):
-        values = jnp.concatenate(
+    def stack_pair(reals, imags):
+        return jnp.concatenate(
             [jnp.concatenate(reals, axis=1), jnp.concatenate(imags, axis=1)], axis=0
         )
-        mixed = product3(square_pair(matrices, 0), parts(values), NN)
+
+    def work_columns(groups):
+        members = [member for group in groups for member in group]
         cosine = floats[SPIN_AT : SPIN_AT + 128, :]
         sine = floats[SPIN_AT + 128 : SPIN_AT + 256, :]
+        loaded = [
+            stack_pair(
+                [columns[column_rows(REAL_ROWS[member]), :] for member in group],
+                [columns[column_rows(IMAG_ROWS[member]), :] for member in group],
+            )
+            for group in groups
+        ]
         turned = []
-        for index in range(len(members)):
-            real, imag = mixed[:128, plane(index)], mixed[128:, plane(index)]
-            turned.append(
-                jnp.concatenate([real * cosine + imag * sine, imag * cosine - real * sine], axis=1)
-            )
-        turned = jnp.concatenate(turned, axis=0)
-        modes = product3(parts(turned), square_pair(matrices, 2), NN)
+        for group, values in zip(groups, loaded):
+            mixed = product3(square_pair(matrices, 0), parts(values), NN)
+            for index in range(len(group)):
+                real, imag = mixed[:128, plane(index)], mixed[128:, plane(index)]
+                turned.append(
+                    jnp.concatenate(
+                        [real * cosine + imag * sine, imag * cosine - real * sine], axis=1
+                    )
+                )
+        modes = product3(
+            parts(jnp.concatenate(turned, axis=0)), square_pair(matrices, 2), NN
+        )
         changed = []
         for index, member in enumerate(members):
             piece = modes[plane(index)]
             real, imag = apply_gains(gains, member, piece[:, :128], piece[:, 128:])
             changed.append(jnp.concatenate([real, imag], axis=1))
-        changed = jnp.concatenate(changed, axis=0)
-        mixed = product3(parts(changed), square_pair(matrices, 3), NN)
-        reals, imags = [], []
-        for index in range(len(members)):
-            piece = mixed[plane(index)]
-            real, imag = piece[:, :128], piece[:, 128:]
-            reals.append(real * cosine - imag * sine)
-            imags.append(imag * cosine + real * sine)
-        values = jnp.concatenate(
-            [jnp.concatenate(reals, axis=1), jnp.concatenate(imags, axis=1)], axis=0
+        mixed = product3(
+            parts(jnp.concatenate(changed, axis=0)), square_pair(matrices, 3), NN
         )
-        values = product3(square_pair(matrices, 1), parts(values), NN)
-        return [
-            (values[:128, plane(index)], values[128:, plane(index)])
-            for index in range(len(members))
-        ]
-
-    def work_columns(groups):
-        loaded = [
-            [
-                [columns[column_rows(rows[member]), :] for member in group]
-                for rows in (REAL_ROWS, IMAG_ROWS)
-            ]
-            for group in groups
-        ]
-        done = [column_math(group, *values) for group, values in zip(groups, loaded)]
-        for group, results_of in zip(groups, done):
-            for member, (real, imag) in zip(group, results_of):
-                columns[column_rows(REAL_ROWS[member]), :] = real
-                columns[column_rows(IMAG_ROWS[member]), :] = imag
+        start = 0
+        done = []
+        for group in groups:
+            reals, imags = [], []
+            for index in range(start, start + len(group)):
+                piece = mixed[plane(index)]
+                real, imag = piece[:, :128], piece[:, 128:]
+                reals.append(real * cosine - imag * sine)
+                imags.append(imag * cosine + real * sine)
+            start += len(group)
+            done.append(
+                product3(square_pair(matrices, 1), parts(stack_pair(reals, imags)), NN)
+            )
+        for group, values in zip(groups, done):
+            for index, member in enumerate(group):
+                columns[column_rows(REAL_ROWS[member]), :] = values[:128, plane(index)]
+                columns[column_rows(IMAG_ROWS[member]), :] = values[128:, plane(index)]
 
     def collect(side, slot):
         first = 0 if side == 0 else FIRST
@@ -623,31 +647,48 @@
         keep_own(side, returned, sem_back_in)
 
     lax.fori_loop(0, steps, spread(0), 0)
+    columns[column_rows(FIRST - 1), :] = jnp.zeros((128, 128), F32)
     work_columns([(0, 1), (2, 3), (4, 5)])
     lax.fori_loop(0, steps, spread(1), 0)
+    columns[column_rows(SLAB - 1), :] = jnp.zeros((128, 128), F32)
     work_columns([(6, 7)])
     send_back(0)
     work_columns([(8, 9), (10,)])
     send_back(1)
 
-    def wave_body(step, carry):
-        slots = slots_before(step)
-        for side in range(2):
-            for slot in slots:
-                wait_group(side, slot, returned, sem_back_in)
+    def wave_part(side, slots):
+        start = INV_AT if side == 0 else INV_AT + GX * FIRST
+        count = GX * FIRST if side == 0 else GX * (SLAB - FIRST)
         loaded = [
             (
-                [returned[pl.ds(slot * GX, GX), sides[side]] for side in range(2)],
-                matrix_pair(matrices, INV_AT, jnp.minimum(slot, 1)),
-                floats[pl.ds(32 * slot, 1), :],
-                floats[pl.ds(32 * slot + 16, 1), :],
+                returned[pl.ds(slot * GX, GX), sides[side]],
+                matrix_pair(matrices, start, jnp.minimum(slot, 1), count),
             )
             for slot in slots
         ]
+        return [
+            product3(parts(decode(codes).reshape(count, 128)), right, TN)
+            for codes, right in loaded
+        ]
+
+    def first_wave(step, carry):
+        slots = slots_before(step)
+        for slot in slots:
+            wait_group(0, slot, returned, sem_back_in)
+        for slot, values in zip(slots, wave_part(0, slots)):
+            waves[slot] = values
+        return carry
+
+    def second_wave(step, carry):
+        slots = slots_before(step)
+        for slot in slots:
+            wait_group(1, slot, returned, sem_back_in)
+        before = [waves[slot] for slot in slots]
         done = []
-        for codes, right, cosine, sine in loaded:
-            block = jnp.concatenate([decode(code) for code in codes], axis=1)
-            values = product3(parts(block.reshape(GX * SLAB, 128)), right, TN)
+        for slot, values, base in zip(slots, wave_part(1, slots), before):
+            values = values + base
+            cosine = floats[pl.ds(32 * slot, 1), :]
+            sine = floats[pl.ds(32 * slot + 16, 1), :]
             real, imag = values[:, :128], values[:, 128:]
             done.append((real * cosine - imag * sine, imag * cosine + real * sine))
         for slot, (real, imag) in zip(slots, done):
@@ -655,7 +696,8 @@
             waves[slot, :, 128:256] = imag
         return carry
 
-    lax.fori_loop(0, steps, wave_body, 0)
+    lax.fori_loop(0, steps, first_wave, 0)
+    lax.fori_loop(0, steps, second_wave, 0)
 
     def grid_body(step, carry):
         field = step // 2

time: 69.9 us -> 67.1 us (0.960)
  Pallas kernels: 69.1 us -> 66.3 us
    pallas_call x1, Pallas kernels: 68.1 us -> 65.3 us  [per_device(): pl.pallas_call(step_kernel, out_shape=(block,) * 4, in_specs=[pl.BlockSpe...]
where the time goes in v4:
time: 67.1 us; the launch traced here: 67 us
  Pallas kernels  66.3 us (99%)
    pallas_call x1, Pallas kernels, per_device(): pl.pallas_call(step_kernel, out_shape=(block,) * 4, in_specs=[pl.BlockSpe...  65.3 us

profile of v4, /device:TPU:1, one launch (start us, length us, event | category | flops | bytes accessed | tf_op | source)
XLA Modules:
  0.0 67.0 jit_solution(6222951651974553843)
XLA Ops:
  0.6 65.3 %shard_map.93 = (bf16[256,512]{1,0:T(8,128)(2,1)S(1)}, bf16[256,512]{1,0:T(8,128)(2,1)S(1)}, bf16[256,512]{1,0:T(8,128)(2,1)S(1)}, bf16[256,512]{1,0:T(8,128)(2,1)S(1)}) custom-call(bf16[256,512]{1,0:T(8,128)(2,1)} %refs_0_.1, bf16[256,512]{1,0:T(8,128)(2,1)} %refs_1_.1, bf16[256,512]{1,0:T(8,128)(2,1)} %refs_2_.1, bf16[256,512]{1,0:T(8,128)(2,1)} %refs_3_.1, ...), custom_call_target="tpu_custom_call" | custom-call | tf_op jit(solution)/shard_map/pallas_call | solution.py:756
  66.0 1.0 %shard_map.94 = (bf16[256,512]{1,0:T(8,128)(2,1)}, bf16[256,512]{1,0:T(8,128)(2,1)}, bf16[256,512]{1,0:T(8,128)(2,1)}, bf16[256,512]{1,0:T(8,128)(2,1)}) custom-call(bf16[256,512]{1,0:T(8,128)(2,1)S(1)} %get-tuple-element.8.refs_0_, bf16[256,512]{1,0:T(8,128)(2,1)S(1)} %get-tuple-element.9.refs_1_, bf16[256,512]{1,0:T(8,128)(2,1)S(1)} %get-tuple-element.10.refs_2_, ...), custom_call_target="tpu_custom_call" | custom-call | tf_op jit(solution)/shard_map/pallas_call | solution.py:793

commit v5 on v4

--- a/solution.py
+++ b/solution.py
@@ -415,7 +415,7 @@
             pltpu.make_async_remote_copy(
                 src_ref=sources[field].at[pl.ds(pl.multiple_of(other * ROWS, ROWS), ROWS), :],
                 dst_ref=grid_rows.at[field, octant],
-                send_sem=sem_rows_out.at[field],
+                send_sem=sem_rows_out,
                 recv_sem=sem_rows_in.at[field],
                 device_id=(other, slot_own),
                 device_id_type=MESH,
@@ -485,19 +485,22 @@
                 src_ref=slabs.at[slot * GX + other, sides[side]],
                 dst_ref=target.at[own, sides[side]],
                 send_sem=out_sem.at[side],
-                recv_sem=in_sem.at[side, slot_own],
+                recv_sem=in_sem.at[side, slot_own // 2],
                 device_id=(other, slot),
                 device_id_type=MESH,
             ).start()
 
     def keep_own(side, target, in_sem):
         pltpu.make_async_copy(
-            slabs.at[own, sides[side]], target.at[own, sides[side]], in_sem.at[side, slot_own]
+            slabs.at[own, sides[side]],
+            target.at[own, sides[side]],
+            in_sem.at[side, slot_own // 2],
         ).start()
 
-    def wait_group(side, slot, target, in_sem):
-        group = target.at[pl.ds(slot * GX, GX), sides[side]]
-        pltpu.make_async_copy(group, group, in_sem.at[side, slot]).wait()
+    def wait_group(side, slots, target, in_sem):
+        couple = slots[0] // 2
+        group = target.at[pl.ds(couple * (2 * GX), 2 * GX), sides[side]]
+        pltpu.make_async_copy(group, group, in_sem.at[side, couple]).wait()
 
     def wait_sent(side, out_sem):
         sent = slabs.at[pl.ds(0, DEVICES - 1), sides[side]]
@@ -519,15 +522,18 @@
     steps = GY // 2
 
     def slot_body(step, carry):
-        slots = slots_at(step)
+        slots = slots_at(2 * step) + slots_at(2 * step + 1)
         slot_products(slots)
         for slot in slots:
             send_slot(0, slot, octants, landed, sem_out, sem_in)
         return carry
 
-    lax.fori_loop(0, steps - 1, slot_body, 0)
+    lax.fori_loop(0, steps // 2 - 1, slot_body, 0)
     twin = slots_at(steps - 1)[0]
-    slot_products([twin, slot_own])
+    nearby = slots_at(steps - 2)
+    slot_products(nearby + [twin, slot_own])
+    for slot in nearby:
+        send_slot(0, slot, octants, landed, sem_out, sem_in)
     send_slot(0, twin, octants, landed, sem_out, sem_in)
     send_slot(0, slot_own, octants[:-1], landed, sem_out, sem_in)
     keep_own(0, landed, sem_in)
@@ -547,8 +553,9 @@
         count = FIRST if side == 0 else SLAB - FIRST
 
         def body(step, carry):
-            for slot in slots_before(step):
-                wait_group(side, slot, landed, sem_in)
+            slots = slots_before(step)
+            wait_group(side, slots, landed, sem_in)
+            for slot in slots:
                 values = decode(landed[pl.ds(slot * GX, GX), sides[side]])
                 for source in range(GX):
                     columns[
@@ -619,30 +626,37 @@
                 columns[column_rows(REAL_ROWS[member]), :] = values[:128, plane(index)]
                 columns[column_rows(IMAG_ROWS[member]), :] = values[128:, plane(index)]
 
-    def collect(side, slot):
+    def collect(side, slots):
         first = 0 if side == 0 else FIRST
         count = FIRST if side == 0 else SLAB - FIRST
-        values = jnp.stack(
-            [
-                columns[pl.ds(first * PLANE + slot * GX + source, count, stride=PLANE), :]
-                for source in range(GX)
-            ]
-        )
-        slabs[pl.ds(slot * GX, GX), sides[side]] = encode(values)
+        codes = [
+            encode(
+                jnp.stack(
+                    [
+                        columns[
+                            pl.ds(first * PLANE + slot * GX + source, count, stride=PLANE), :
+                        ]
+                        for source in range(GX)
+                    ]
+                )
+            )
+            for slot in slots
+        ]
+        for slot, code in zip(slots, codes):
+            slabs[pl.ds(slot * GX, GX), sides[side]] = code
 
     def send_back(side):
         def body(step, carry):
             slots = slots_at(step)
+            collect(side, slots)
             for slot in slots:
-                collect(side, slot)
                 send_slot(side, slot, octants, returned, sem_back_out, sem_back_in)
             return carry
 
         wait_sent(side, sem_out)
         lax.fori_loop(0, steps - 1, body, 0)
-        collect(side, twin)
+        collect(side, [twin, slot_own])
         send_slot(side, twin, octants, returned, sem_back_out, sem_back_in)
-        collect(side, slot_own)
         send_slot(side, slot_own, octants[:-1], returned, sem_back_out, sem_back_in)
         keep_own(side, returned, sem_back_in)
 
@@ -672,17 +686,21 @@
         ]
 
     def first_wave(step, carry):
-        slots = slots_before(step)
-        for slot in slots:
-            wait_group(0, slot, returned, sem_back_in)
+        slots = []
+        for index in (2 * step, 2 * step + 1):
+            couple = slots_before(index)
+            wait_group(0, couple, returned, sem_back_in)
+            slots.extend(couple)
         for slot, values in zip(slots, wave_part(0, slots)):
             waves[slot] = values
         return carry
 
     def second_wave(step, carry):
-        slots = slots_before(step)
-        for slot in slots:
-            wait_group(1, slot, returned, sem_back_in)
+        slots = []
+        for index in (2 * step, 2 * step + 1):
+            couple = slots_before(index)
+            wait_group(1, couple, returned, sem_back_in)
+            slots.extend(couple)
         before = [waves[slot] for slot in slots]
         done = []
         for slot, values, base in zip(slots, wave_part(1, slots), before):
@@ -696,8 +714,8 @@
             waves[slot, :, 128:256] = imag
         return carry
 
-    lax.fori_loop(0, steps, first_wave, 0)
-    lax.fori_loop(0, steps, second_wave, 0)
+    lax.fori_loop(0, steps // 2, first_wave, 0)
+    lax.fori_loop(0, steps // 2, second_wave, 0)
 
     def grid_body(step, carry):
         field = step // 2
@@ -719,7 +737,7 @@
             pltpu.make_async_remote_copy(
                 src_ref=new_rows.at[field, other],
                 dst_ref=results[field].at[own_rows, :],
-                send_sem=sem_last_out.at[field],
+                send_sem=sem_last_out,
                 recv_sem=sem_last_in.at[field],
                 device_id=(other, slot_own),
                 device_id_type=MESH,
@@ -730,10 +748,10 @@
 
     for side in range(2):
         wait_sent(side, sem_back_out)
+    moved = new_rows.at[:, pl.ds(0, GX - 1)]
+    pltpu.make_async_copy(moved, moved, sem_rows_out).wait()
+    pltpu.make_async_copy(moved, moved, sem_last_out).wait()
     for field in range(FIELDS):
-        moved = new_rows.at[field, pl.ds(0, GX - 1)]
-        pltpu.make_async_copy(moved, moved, sem_rows_out.at[field]).wait()
-        pltpu.make_async_copy(moved, moved, sem_last_out.at[field]).wait()
         pltpu.make_async_copy(results[field], results[field], sem_last_in.at[field]).wait()
 
 
@@ -766,19 +784,19 @@
             pltpu.VMEM((GY, 128, 256), BF16),
             pltpu.VMEM((DEVICES, SLAB // 8, 8, 128), BF16),
             pltpu.VMEM((DEVICES, SLAB // 8, 8, 128), BF16),
-            pltpu.VMEM((SLAB * PLANE, 128), F32),
+            pltpu.VMEM(((SLAB + 1) * PLANE, 128), F32),
             pltpu.VMEM((KX, 4, 128, 128), F32),
             pltpu.VMEM((DEVICES, SLAB // 8, 8, 128), BF16),
             pltpu.VMEM((GY, 128, 256), F32),
             pltpu.VMEM((FIELDS, GX, ROWS, COLS), BF16),
             dma((2,)),
-            dma((FIELDS,)),
+            dma,
             dma((FIELDS,)),
             dma((2,)),
-            dma((2, GY)),
+            dma((2, GY // 2)),
             dma((2,)),
-            dma((2, GY)),
-            dma((FIELDS,)),
+            dma((2, GY // 2)),
+            dma,
             dma((FIELDS,)),
             pltpu.SemaphoreType.REGULAR,
             pltpu.SemaphoreType.REGULAR,

time: 67.1 us -> 65.1 us (0.970)
  Pallas kernels: 66.3 us -> 64.4 us
    pallas_call x1, Pallas kernels: 65.3 us -> 63.4 us  [per_device(): pl.pallas_call(step_kernel, out_shape=(block,) * 4, in_specs=[pl.BlockSpe...]
where the time goes in v5:
time: 65.1 us; the launch traced here: 65 us
  Pallas kernels  64.4 us (99%)
    pallas_call x1, Pallas kernels, per_device(): pl.pallas_call(step_kernel, out_shape=(block,) * 4, in_specs=[pl.BlockSpe...  63.4 us

profile of v5, /device:TPU:1, one launch (start us, length us, event | category | flops | bytes accessed | tf_op | source)
XLA Modules:
  0.0 65.0 jit_solution(5509545922606601811)
XLA Ops:
  0.6 63.4 %shard_map.93 = (bf16[256,512]{1,0:T(8,128)(2,1)S(1)}, bf16[256,512]{1,0:T(8,128)(2,1)S(1)}, bf16[256,512]{1,0:T(8,128)(2,1)S(1)}, bf16[256,512]{1,0:T(8,128)(2,1)S(1)}) custom-call(bf16[256,512]{1,0:T(8,128)(2,1)} %refs_0_.1, bf16[256,512]{1,0:T(8,128)(2,1)} %refs_1_.1, bf16[256,512]{1,0:T(8,128)(2,1)} %refs_2_.1, bf16[256,512]{1,0:T(8,128)(2,1)} %refs_3_.1, ...), custom_call_target="tpu_custom_call" | custom-call | tf_op jit(solution)/shard_map/pallas_call | solution.py:774
  64.0 1.0 %shard_map.94 = (bf16[256,512]{1,0:T(8,128)(2,1)}, bf16[256,512]{1,0:T(8,128)(2,1)}, bf16[256,512]{1,0:T(8,128)(2,1)}, bf16[256,512]{1,0:T(8,128)(2,1)}) custom-call(bf16[256,512]{1,0:T(8,128)(2,1)S(1)} %get-tuple-element.8.refs_0_, bf16[256,512]{1,0:T(8,128)(2,1)S(1)} %get-tuple-element.9.refs_1_, bf16[256,512]{1,0:T(8,128)(2,1)S(1)} %get-tuple-element.10.refs_2_, ...), custom_call_target="tpu_custom_call" | custom-call | tf_op jit(solution)/shard_map/pallas_call | solution.py:811

commit v6 on v5

--- a/solution.py
+++ b/solution.py
@@ -21,7 +21,8 @@
 IMAG_ROWS = (8, 9, 10, 11, 12, 13, 14, 16, 20, 21, 22)
 ROWS = 32
 COLS = 512
-POWER = 11
+POWER = 17
+PEAK = 128.0
 
 coriolis = 0.25
 gravity_step = 2.0
@@ -120,11 +121,11 @@
     rows = values.shape[1]
     largest = jnp.max(jnp.abs(values), axis=1, keepdims=True)
     scale = (jnp.maximum(largest, 1e-34) * 1.01).astype(BF16).astype(F32)
-    level = values * (2048.0 / scale)
+    level = values * (PEAK / scale)
     second = level * level
     fourth = second * second
     eighth = fourth * fourth
-    code = eighth * second * level
+    code = eighth * eighth * level
     ending = code[:, rows - 8 :]
     last = lax.broadcasted_iota(jnp.int32, ending.shape, 1) == 7
     ending = jnp.where(last, scale, ending)
@@ -135,7 +136,7 @@
 def decode(codes):
     rows = codes.shape[1] * 8
     code = codes.astype(F32).reshape(codes.shape[0], rows, 128)
-    scale = code[:, rows - 1 : rows, :] * (1.0 / 2048.0)
+    scale = code[:, rows - 1 : rows, :] * (1.0 / PEAK)
     size = jnp.maximum(jnp.abs(code), 2.0**-126)
     return jnp.exp2(jnp.log2(size) * (1.0 / POWER - 1.0)) * (code * scale)
 

time: 65.1 us -> 65.1 us (level)
  no operation moved by 1% of the time
where the time goes in v6:
time: 65.1 us; the launch traced here: 65 us
  Pallas kernels  64.4 us (99%)
    pallas_call x1, Pallas kernels, per_device(): pl.pallas_call(step_kernel, out_shape=(block,) * 4, in_specs=[pl.BlockSpe...  63.4 us

profile of v6, /device:TPU:1, one launch (start us, length us, event | category | flops | bytes accessed | tf_op | source)
XLA Modules:
  0.0 65.0 jit_solution(15454504291646629556)
XLA Ops:
  0.6 63.4 %shard_map.93 = (bf16[256,512]{1,0:T(8,128)(2,1)S(1)}, bf16[256,512]{1,0:T(8,128)(2,1)S(1)}, bf16[256,512]{1,0:T(8,128)(2,1)S(1)}, bf16[256,512]{1,0:T(8,128)(2,1)S(1)}) custom-call(bf16[256,512]{1,0:T(8,128)(2,1)} %refs_0_.1, bf16[256,512]{1,0:T(8,128)(2,1)} %refs_1_.1, bf16[256,512]{1,0:T(8,128)(2,1)} %refs_2_.1, bf16[256,512]{1,0:T(8,128)(2,1)} %refs_3_.1, ...), custom_call_target="tpu_custom_call" | custom-call | tf_op jit(solution)/shard_map/pallas_call | solution.py:775
  64.0 1.0 %shard_map.94 = (bf16[256,512]{1,0:T(8,128)(2,1)}, bf16[256,512]{1,0:T(8,128)(2,1)}, bf16[256,512]{1,0:T(8,128)(2,1)}, bf16[256,512]{1,0:T(8,128)(2,1)}) custom-call(bf16[256,512]{1,0:T(8,128)(2,1)S(1)} %get-tuple-element.8.refs_0_, bf16[256,512]{1,0:T(8,128)(2,1)S(1)} %get-tuple-element.9.refs_1_, bf16[256,512]{1,0:T(8,128)(2,1)S(1)} %get-tuple-element.10.refs_2_, ...), custom_call_target="tpu_custom_call" | custom-call | tf_op jit(solution)/shard_map/pallas_call | solution.py:812

commit v7 on v6

--- a/solution.py
+++ b/solution.py
@@ -21,8 +21,8 @@
 IMAG_ROWS = (8, 9, 10, 11, 12, 13, 14, 16, 20, 21, 22)
 ROWS = 32
 COLS = 512
-POWER = 17
-PEAK = 128.0
+POWER = 15
+PEAK = 256.0
 
 coriolis = 0.25
 gravity_step = 2.0
@@ -125,7 +125,7 @@
     second = level * level
     fourth = second * second
     eighth = fourth * fourth
-    code = eighth * eighth * level
+    code = eighth * fourth * (second * level)
     ending = code[:, rows - 8 :]
     last = lax.broadcasted_iota(jnp.int32, ending.shape, 1) == 7
     ending = jnp.where(last, scale, ending)

time: 65.1 us -> 66.2 us (1.017)
  Pallas kernels: 64.4 us -> 65.4 us
    pallas_call x1, Pallas kernels: 63.4 us -> 64.4 us  [per_device(): pl.pallas_call(step_kernel, out_shape=(block,) * 4, in_specs=[pl.BlockSpe...]
where the time goes in v7:
time: 66.2 us; the launch traced here: 66.1 us
  Pallas kernels  65.4 us (99%)
    pallas_call x1, Pallas kernels, per_device(): pl.pallas_call(step_kernel, out_shape=(block,) * 4, in_specs=[pl.BlockSpe...  64.4 us

profile of v7, /device:TPU:1, one launch (start us, length us, event | category | flops | bytes accessed | tf_op | source)
XLA Modules:
  0.0 66.1 jit_solution(15441487167760222007)
XLA Ops:
  0.6 64.4 %shard_map.93 = (bf16[256,512]{1,0:T(8,128)(2,1)S(1)}, bf16[256,512]{1,0:T(8,128)(2,1)S(1)}, bf16[256,512]{1,0:T(8,128)(2,1)S(1)}, bf16[256,512]{1,0:T(8,128)(2,1)S(1)}) custom-call(bf16[256,512]{1,0:T(8,128)(2,1)} %refs_0_.1, bf16[256,512]{1,0:T(8,128)(2,1)} %refs_1_.1, bf16[256,512]{1,0:T(8,128)(2,1)} %refs_2_.1, bf16[256,512]{1,0:T(8,128)(2,1)} %refs_3_.1, ...), custom_call_target="tpu_custom_call" | custom-call | tf_op jit(solution)/shard_map/pallas_call | solution.py:775
  65.1 1.0 %shard_map.94 = (bf16[256,512]{1,0:T(8,128)(2,1)}, bf16[256,512]{1,0:T(8,128)(2,1)}, bf16[256,512]{1,0:T(8,128)(2,1)}, bf16[256,512]{1,0:T(8,128)(2,1)}) custom-call(bf16[256,512]{1,0:T(8,128)(2,1)S(1)} %get-tuple-element.8.refs_0_, bf16[256,512]{1,0:T(8,128)(2,1)S(1)} %get-tuple-element.9.refs_1_, bf16[256,512]{1,0:T(8,128)(2,1)S(1)} %get-tuple-element.10.refs_2_, ...), custom_call_target="tpu_custom_call" | custom-call | tf_op jit(solution)/shard_map/pallas_call | solution.py:812

commit v8 on v6

--- a/solution.py
+++ b/solution.py
@@ -698,7 +698,7 @@
 
     def second_wave(step, carry):
         slots = []
-        for index in (2 * step, 2 * step + 1):
+        for index in (4 * step, 4 * step + 1, 4 * step + 2, 4 * step + 3):
             couple = slots_before(index)
             wait_group(1, couple, returned, sem_back_in)
             slots.extend(couple)
@@ -716,7 +716,7 @@
         return carry
 
     lax.fori_loop(0, steps // 2, first_wave, 0)
-    lax.fori_loop(0, steps // 2, second_wave, 0)
+    lax.fori_loop(0, steps // 4, second_wave, 0)
 
     def grid_body(step, carry):
         field = step // 2

time: 65.1 us -> 65.8 us (1.011)
  no operation moved by 1% of the time
where the time goes in v8:
time: 65.8 us; the launch traced here: 65.7 us
  Pallas kernels  65 us (99%)
    pallas_call x1, Pallas kernels, per_device(): pl.pallas_call(step_kernel, out_shape=(block,) * 4, in_specs=[pl.BlockSpe...  64 us

profile of v8, /device:TPU:1, one launch (start us, length us, event | category | flops | bytes accessed | tf_op | source)
XLA Modules:
  0.0 65.7 jit_solution(12928885615817223167)
XLA Ops:
  0.6 64.0 %shard_map.93 = (bf16[256,512]{1,0:T(8,128)(2,1)S(1)}, bf16[256,512]{1,0:T(8,128)(2,1)S(1)}, bf16[256,512]{1,0:T(8,128)(2,1)S(1)}, bf16[256,512]{1,0:T(8,128)(2,1)S(1)}) custom-call(bf16[256,512]{1,0:T(8,128)(2,1)} %refs_0_.1, bf16[256,512]{1,0:T(8,128)(2,1)} %refs_1_.1, bf16[256,512]{1,0:T(8,128)(2,1)} %refs_2_.1, bf16[256,512]{1,0:T(8,128)(2,1)} %refs_3_.1, ...), custom_call_target="tpu_custom_call" | custom-call | tf_op jit(solution)/shard_map/pallas_call | solution.py:775
  64.7 1.0 %shard_map.94 = (bf16[256,512]{1,0:T(8,128)(2,1)}, bf16[256,512]{1,0:T(8,128)(2,1)}, bf16[256,512]{1,0:T(8,128)(2,1)}, bf16[256,512]{1,0:T(8,128)(2,1)}) custom-call(bf16[256,512]{1,0:T(8,128)(2,1)S(1)} %get-tuple-element.8.refs_0_, bf16[256,512]{1,0:T(8,128)(2,1)S(1)} %get-tuple-element.9.refs_1_, bf16[256,512]{1,0:T(8,128)(2,1)S(1)} %get-tuple-element.10.refs_2_, ...), custom_call_target="tpu_custom_call" | custom-call | tf_op jit(solution)/shard_map/pallas_call | solution.py:812
